TPU v7x, 32 devices: a whole 2x2x4 slice. The times are simulated.
32 devices in a mesh: seq: 16 (over z, y, x), tp: 2 (over core).
Axes of the slice: x: 2, y: 2, z: 4, core: 2. Of those that a mesh axis runs over, the one named last changes fastest.
Arguments:
- inputs: bfloat16 [16384, 768], P('seq'), may hold values from -6 to 6
- cotangent: bfloat16 [16384, 768], P('seq'), may hold values from -6 to 6
- query_weight: bfloat16 [768, 768], P(None, 'tp'), may hold values from -0.21875 to 0.21875
- key_weight: bfloat16 [768, 768], P(None, 'tp'), may hold values from -0.21875 to 0.21875
- value_weight: bfloat16 [768, 768], P(None, 'tp'), may hold values from -0.21875 to 0.21875
- out_weight: bfloat16 [768, 768], P('tp'), may hold values from -0.21875 to 0.21875
- up_weight: bfloat16 [768, 3072], P(None, 'tp'), may hold values from -0.21875 to 0.21875
- down_weight: bfloat16 [3072, 768], P('tp'), may hold values from -0.21875 to 0.21875
- conv_taps: float32 [12, 33], P('tp'), may hold values from -1 to 1
- attn_gain: float32 [768], replicated, may hold values from 0.5 to 1.5
- attn_shift: float32 [768], replicated, may hold values from -1 to 1
- ffn_gain: float32 [768], replicated, may hold values from 0.5 to 1.5
- ffn_shift: float32 [768], replicated, may hold values from -1 to 1
- hyperplanes: bfloat16 [32, 8, 64], replicated, may hold values from -6 to 6
- lengths: int32 [32], replicated, may hold values from 1 to 4096, 16384 in all
Outputs:
- output: bfloat16 [16384, 768], P('seq')
- grad_inputs: float32 [16384, 768], P('seq')
- grad_query: float32 [768, 768], P(None, 'tp')
- grad_key: float32 [768, 768], P(None, 'tp')
- grad_value: float32 [768, 768], P(None, 'tp')
- grad_out: float32 [768, 768], P('tp')
- grad_up: float32 [768, 3072], P(None, 'tp')
- grad_down: float32 [3072, 768], P('tp')
- grad_taps: float32 [12, 33], P('tp')
- grad_attn_gain: float32 [768], replicated
- grad_attn_shift: float32 [768], replicated
- grad_ffn_gain: float32 [768], replicated
- grad_ffn_shift: float32 [768], replicated
- occupancy: float32 [12, 32, 256], P('tp')
Inputs may be any that keep to these rules, and one draw needn't show every extreme that they name: The 32 lengths sum to 16384, and the longest is exactly 4096; sequences lie one after another along the tokens.
All inputs are finite; a program needn't handle non-finite values.
Results may differ from a plain program's by a relative error of at most 0.018.
Values may be sent and summed in bfloat16 or wider, within the bound.
A program may use at most 256 MiB of HBM per device.

v0:
```python
from functools import partial
import math

import jax
import jax.numpy as jnp
from jax import lax
from jax.experimental import pallas as pl
from jax.experimental.pallas import tpu as pltpu
from jax.sharding import PartitionSpec as P

TAU = 8
BITS = 8
CONV = 33
MOST = 4096
RIM = (CONV - 1) // 2

EPS_UNIT = 1e-06
EPS_LAYER = 1e-05
SHARP = 4.0
CLIP_EDGE = 0.999

CHUNK = 512
Q_TILE = 512
Q_TILE_BACK = 256
PAIR = 128
STRIP = 128
FAR_ID = 1 << 20

LIGHT = pl.CostEstimate(flops=1 << 20, bytes_accessed=1 << 16, transcendentals=0)

F32 = jnp.float32
BF16 = jnp.bfloat16

ARC = (
    0.49999961256980896,
    -0.06828052550554276,
    0.027964841574430466,
    -0.014291195198893547,
    0.006136968266218901,
    -0.001371906721033156,
)


def params(**kwargs):
    return pltpu.CompilerParams(vmem_limit_bytes=56 << 20, **kwargs)


def nn(left, right):
    return lax.dot_general(left, right, (((1,), (0,)), ((), ())), preferred_element_type=F32)


def nt(left, right):
    return lax.dot_general(left, right, (((1,), (1,)), ((), ())), preferred_element_type=F32)


def tn(left, right):
    return lax.dot_general(left, right, (((0,), (0,)), ((), ())), preferred_element_type=F32)


def head_masks(head_dim):
    lanes = lax.broadcasted_iota(jnp.int32, (1, PAIR), 1)
    first = (lanes < head_dim).astype(F32)
    return first.astype(BF16), (1.0 - first).astype(BF16)


def head_sum(rows, head_dim):
    here = lax.broadcasted_iota(jnp.int32, (PAIR, PAIR), 0) // head_dim
    there = lax.broadcasted_iota(jnp.int32, (PAIR, PAIR), 1) // head_dim
    ones = (here == there).astype(F32).astype(BF16)
    sums = []
    for start in range(0, rows.shape[1], PAIR):
        part = rows[:, start : start + PAIR]
        high = part.astype(BF16)
        low = (part - high.astype(F32)).astype(BF16)
        sums.append(nn(high, ones) + nn(low, ones))
    return jnp.concatenate(sums, axis=1)


def pick_half(mine_refs, other_ref, kept):
    step = pl.program_id(0)
    for index, ref in enumerate(mine_refs):

        @pl.when(step == index)
        def _():
            kept[...] = ref[...]

    @pl.when(step >= len(mine_refs))
    def _():
        kept[...] = other_ref[...]


def other_spec(count, shape):
    return pl.BlockSpec(shape, lambda i, t: (jnp.maximum(i - count, 0), 0))


def half_specs(count, shape):
    return [pl.BlockSpec(shape, lambda i, t: (0, 0))] * count + [other_spec(count, shape)]


def project_kernel(units, count, head_dim, table, *refs):
    if count:
        mine_refs, other_ref, w_ref = refs[:count], refs[count], refs[count + 1]
        out_refs, kept = refs[count + 2 : -1], refs[-1]
        pick_half(mine_refs, other_ref, kept)
    else:
        kept, w_ref = refs[:2]
        out_refs = refs[2:]
    width = out_refs[-1].shape[1]
    needed = table[pl.num_programs(0) + pl.program_id(0)] > 0

    @pl.when(needed)
    def _():
        whole = nn(kept[...], w_ref[...])
        for index in range(units):
            part = whole[:, index * width : (index + 1) * width]
            scale = lax.rsqrt(head_sum(part * part, head_dim) * (1.0 / head_dim) + EPS_UNIT)
            scale = scale * (1.0 / math.sqrt(head_dim))
            out_refs[2 * index][...] = (part * scale).astype(BF16)
            out_refs[2 * index + 1][...] = scale
        out_refs[-1][...] = whole[:, units * width :].astype(BF16)


def project(table, halves, weight, units, head_dim, chunks=None):
    depth = halves[0].shape[1]
    rows = sum(h.shape[0] for h in halves)
    count = len(halves) - 1
    width = weight.shape[1] // (units + 1)
    row_spec = pl.BlockSpec((CHUNK, width), lambda i, t: (t[i], 0))
    held = (chunks + 1) * CHUNK if count else rows
    if count:
        x_specs = half_specs(count, (CHUNK, depth))
    else:
        x_specs = [pl.BlockSpec((CHUNK, depth), lambda i, t: (i, 0))]
    unit_shapes = [
        jax.ShapeDtypeStruct((held, width), BF16),
        jax.ShapeDtypeStruct((held, width), F32),
    ]
    return pl.pallas_call(
        partial(project_kernel, units, count, head_dim),
        grid_spec=pltpu.PrefetchScalarGridSpec(
            num_scalar_prefetch=1,
            grid=(rows // CHUNK,),
            in_specs=x_specs + [pl.BlockSpec(weight.shape, lambda i, t: (0, 0))],
            out_specs=[row_spec] * (2 * units + 1),
            scratch_shapes=[pltpu.VMEM((CHUNK, depth), BF16)] if count else [],
        ),
        out_shape=unit_shapes * units + [jax.ShapeDtypeStruct((held, width), BF16)],
        compiler_params=params(),
        cost_estimate=pl.CostEstimate(
            flops=4 * rows * depth * weight.shape[1], bytes_accessed=rows * depth, transcendentals=0
        ),
        name="project",
    )(table, *halves, weight)


def collide(scores):
    size = jnp.minimum(jnp.abs(scores), CLIP_EDGE)
    rest = 1.0 - size
    poly = ARC[5]
    for factor in ARC[4::-1]:
        poly = poly * size + factor
    angle = (rest * lax.rsqrt(rest)) * poly
    return jnp.where(scores < 0.0, angle, 1.0 - angle)


def tile_facts(table, tiles_q, tiles_k, qi, kt):
    q_low, q_high = table[qi], table[tiles_q + qi]
    k_low, k_high = table[2 * tiles_q + kt], table[2 * tiles_q + tiles_k + kt]
    needed = (k_high >= q_low) & (k_low <= q_high)
    whole = (q_low == q_high) & (k_low == k_high)
    return needed, whole


def id_column(row, lanes):
    column = jnp.broadcast_to(row, (PAIR, row.shape[1])).T
    return jnp.concatenate([column] * (lanes // PAIR), axis=1)


def attend_kernel(
    head_dim, tiles_k, seeded, table, q_ref, qrow_ref, krow_ref, k_ref, v_ref, *rest
):
    out_ref, w_ref = rest[-2:]
    tiles_q = q_ref.shape[0] // Q_TILE
    step, steps = pl.program_id(1), pl.num_programs(1)
    order = 2 * (tiles_q + tiles_k)
    masks = head_masks(head_dim)

    @pl.when(step == 0)
    def _():
        if seeded:
            out_ref[...] = rest[0][...]
        else:
            out_ref[...] = jnp.zeros_like(out_ref)

    @pl.when(step < table[order + steps])
    def _():
        kt = table[order + step]

        def q_loop(qi, carry):
            rows = pl.ds(pl.multiple_of(qi * Q_TILE, Q_TILE), Q_TILE)
            needed, whole = tile_facts(table, tiles_q, tiles_k, qi, kt)

            def part(same):
                q, k = q_ref[rows, :], k_ref[...]
                v_turned = v_ref[...].T
                for index, mask in enumerate(masks):
                    chance = collide(nt(k, q * mask))
                    chance = chance * chance
                    chance = chance * chance
                    chance = chance * chance
                    if same is not None:
                        chance = jnp.where(same, chance, 0.0)
                    weights = chance.astype(BF16)
                    w_ref[index, :, rows] = weights
                    half = slice(index * head_dim, (index + 1) * head_dim)
                    out_ref[half, rows] += nn(v_turned[half, :], weights)

            @pl.when(needed & whole)
            def _():
                part(None)

            @pl.when(needed & jnp.logical_not(whole))
            def _():
                part(id_column(krow_ref[pl.ds(kt, 1), :], Q_TILE) == qrow_ref[pl.ds(qi, 1), :])

            @pl.when(jnp.logical_not(needed))
            def _():
                w_ref[:, :, rows] = jnp.zeros((2, CHUNK, Q_TILE), BF16)

            return carry

        lax.fori_loop(0, tiles_q, q_loop, 0)


def attend(table, q, k, v, qrow, krow, head_dim, seed=None):
    tokens, width = q.shape
    tiles_k = krow.shape[0]
    order = 2 * (tokens // Q_TILE + tiles_k)
    k_spec = pl.BlockSpec((CHUNK, PAIR), lambda p, j, t: (t[order + j], p))
    turned_spec = pl.BlockSpec((PAIR, tokens), lambda p, j, t: (p, 0))
    operands = [q, qrow, krow, k, v]
    specs = [
        pl.BlockSpec((tokens, PAIR), lambda p, j, t: (0, p)),
        pl.BlockSpec(qrow.shape, lambda p, j, t: (0, 0)),
        pl.BlockSpec(krow.shape, lambda p, j, t: (0, 0)),
        k_spec,
        k_spec,
    ]
    if seed is not None:
        operands.append(seed)
        specs.append(turned_spec)
    return pl.pallas_call(
        partial(attend_kernel, head_dim, tiles_k, seed is not None),
        grid_spec=pltpu.PrefetchScalarGridSpec(
            num_scalar_prefetch=1,
            grid=(width // PAIR, tiles_k),
            in_specs=specs,
            out_specs=[
                turned_spec,
                pl.BlockSpec((2, CHUNK, tokens), lambda p, j, t: (p, t[order + j], 0)),
            ],
        ),
        out_shape=[
            jax.ShapeDtypeStruct((width, tokens), F32),
            jax.ShapeDtypeStruct((width // head_dim, tiles_k * CHUNK, tokens), BF16),
        ],
        compiler_params=params(),
        cost_estimate=pl.CostEstimate(
            flops=32 * tokens * tiles_k * CHUNK * width,
            bytes_accessed=tokens * width * 4,
            transcendentals=0,
        ),
        name="attend",
    )(table, *operands)


def back_attend_kernel(
    head_dim, tiles_k, seeded, table, q_ref, g_ref, k_ref, v_ref, w_ref, *rest
):
    dk_ref, dv_ref, dq_ref, acc_k, acc_v = rest[-5:]
    tiles_q = q_ref.shape[0] // Q_TILE_BACK
    step, steps = pl.program_id(1), pl.num_programs(1)
    order = 2 * (tiles_q + tiles_k)
    masks = head_masks(head_dim)

    @pl.when(step == 0)
    def _():
        if seeded:
            dq_ref[...] = rest[0][...]
        else:
            dq_ref[...] = jnp.zeros_like(dq_ref)

    @pl.when(step < table[order + steps])
    def _():
        kt = table[order + step]
        acc_k[...] = jnp.zeros_like(acc_k)
        acc_v[...] = jnp.zeros_like(acc_v)

        def q_loop(qi, carry):
            needed, _ = tile_facts(table, tiles_q, tiles_k, qi, kt)

            @pl.when(needed)
            def _():
                rows = pl.ds(pl.multiple_of(qi * Q_TILE_BACK, Q_TILE_BACK), Q_TILE_BACK)
                q, g, k, v = q_ref[rows, :], g_ref[rows, :], k_ref[...], v_ref[...]
                k_turned = k.T
                sum_k, sum_v = None, None
                for index, mask in enumerate(masks):
                    q_half, g_half = q * mask, g * mask
                    scores = nt(k, q_half)
                    weights = w_ref[index, :, rows]
                    power = jnp.exp(((TAU - 1) / TAU) * jnp.log(weights.astype(F32)))
                    square = scores * scores
                    slope = nt(v, g_half) * (power * lax.rsqrt(1.0 - square))
                    slope = jnp.where(square <= CLIP_EDGE * CLIP_EDGE, slope, 0.0).astype(BF16)
                    term_v = nn(weights, g_half)
                    term_k = nn(slope, q_half)
                    sum_v = term_v if sum_v is None else sum_v + term_v
                    sum_k = term_k if sum_k is None else sum_k + term_k
                    half = slice(index * head_dim, (index + 1) * head_dim)
                    dq_ref[half, rows] += nn(k_turned[half, :], slope)
                acc_v[...] += sum_v
                acc_k[...] += sum_k

            return carry

        lax.fori_loop(0, tiles_q, q_loop, 0)
        dk_ref[...] = acc_k[...].astype(BF16)
        dv_ref[...] = acc_v[...].astype(BF16)


def back_attend(table, tiles_k, q, g, k, v, weights, head_dim, seed=None, cost=LIGHT):
    tokens, width = q.shape
    order = 2 * (tokens // Q_TILE_BACK + tiles_k)
    q_spec = pl.BlockSpec((tokens, PAIR), lambda p, j, t: (0, p))
    k_spec = pl.BlockSpec((CHUNK, PAIR), lambda p, j, t: (t[order + j], p))
    dq_spec = pl.BlockSpec((PAIR, tokens), lambda p, j, t: (p, 0))
    specs = [
        q_spec,
        q_spec,
        k_spec,
        k_spec,
        pl.BlockSpec((2, CHUNK, tokens), lambda p, j, t: (p, t[order + j], 0)),
    ]
    operands = [q, g, k, v, weights]
    if seed is not None:
        operands.append(seed)
        specs.append(dq_spec)
    return pl.pallas_call(
        partial(back_attend_kernel, head_dim, tiles_k, seed is not None),
        grid_spec=pltpu.PrefetchScalarGridSpec(
            num_scalar_prefetch=1,
            grid=(width // PAIR, tiles_k),
            in_specs=specs,
            out_specs=[k_spec, k_spec, dq_spec],
            scratch_shapes=[pltpu.VMEM((CHUNK, PAIR), F32), pltpu.VMEM((CHUNK, PAIR), F32)],
        ),
        out_shape=[
            jax.ShapeDtypeStruct((tiles_k * CHUNK, width), BF16),
            jax.ShapeDtypeStruct((tiles_k * CHUNK, width), BF16),
            jax.ShapeDtypeStruct((width, tokens), F32),
        ],
        compiler_params=params(),
        cost_estimate=cost,
        name="back_attend",
    )(table, *operands)


def back_project_kernel(units, turned, terms, rims, count, head_dim, table, *refs):
    mine_refs, other_ref, w_ref = refs[:count], refs[count], refs[count + 1]
    dx_mine, dx_other, dw_ref, kept, sum_ref = refs[-5:]
    refs = refs[count + 2 : -5]
    step = pl.program_id(0)
    place, needed = table[step], table[pl.num_programs(0) + step] > 0

    @pl.when(step == 0)
    def _():
        dw_ref[...] = jnp.zeros_like(dw_ref)

    def store(value):
        @pl.when(step < count)
        def _():
            dx_mine[...] = value

        @pl.when(step >= count)
        def _():
            dx_other[...] = value

    @pl.when(needed)
    def _():
        pick_half(mine_refs, other_ref, kept)
        grads = []
        for index in range(units):
            unit_ref, scale_ref, grad_ref = refs[3 * index : 3 * index + 3]
            grad = grad_ref[...].astype(F32)
            if index < turned:
                grad = grad.T
            unit = unit_ref[...].astype(F32)
            inner = head_sum(grad * unit, head_dim)
            grads.append(
                ((TAU / math.pi) * scale_ref[...] * (grad - unit * inner)).astype(BF16)
            )
        value_refs = refs[3 * units : 3 * units + terms]
        value = value_refs[0][...].astype(F32)
        for extra in value_refs[1:]:
            value = value + extra[...].astype(F32)
        if rims is not None:
            rim_ref = refs[-1]
            sum_ref[...] = value

            @pl.when(place == rims)
            def _():
                sum_ref[CHUNK - STRIP :, :] += rim_ref[:STRIP, :]

            @pl.when(place == rims + 1)
            def _():
                sum_ref[:STRIP, :] += rim_ref[STRIP:, :]

            value = sum_ref[...]
        grads.append(value.astype(BF16))
        joined = jnp.concatenate(grads, axis=1)
        store(nt(joined, w_ref[...]).astype(BF16))
        dw_ref[...] += tn(kept[...], joined)

    @pl.when(jnp.logical_not(needed))
    def _():
        store(jnp.zeros(dx_mine.shape, BF16))


def back_project(table, halves, weight, parts, turned, values, head_dim, rims=None, rim=None):
    depth = halves[0].shape[1]
    count = len(halves) - 1
    width = values[0].shape[1]
    row_spec = pl.BlockSpec((CHUNK, width), lambda i, t: (t[4 * count + i], 0))
    weight_spec = pl.BlockSpec(weight.shape, lambda i, t: (0, 0))
    wide_specs = [
        pl.BlockSpec((CHUNK, depth), lambda i, t: (jnp.minimum(i, count - 1), 0)),
        other_spec(count, (CHUNK, depth)),
    ]
    specs = half_specs(count, (CHUNK, depth)) + [weight_spec]
    operands = [*halves, weight]
    for index, (unit, scale, grad) in enumerate(parts):
        operands += [unit, scale, grad]
        specs += [row_spec, row_spec]
        specs.append(
            pl.BlockSpec((width, CHUNK), lambda i, t: (0, t[4 * count + i]))
            if index < turned
            else row_spec
        )
    operands += values
    specs += [row_spec] * len(values)
    if rim is not None:
        operands.append(rim)
        specs.append(pl.BlockSpec(rim.shape, lambda i, t: (0, 0)))
    return pl.pallas_call(
        partial(back_project_kernel, len(parts), turned, len(values), rims, count, head_dim),
        grid_spec=pltpu.PrefetchScalarGridSpec(
            num_scalar_prefetch=1,
            grid=(2 * count,),
            in_specs=specs,
            out_specs=wide_specs + [weight_spec],
            scratch_shapes=[pltpu.VMEM((CHUNK, depth), BF16), pltpu.VMEM((CHUNK, width), F32)],
        ),
        out_shape=[
            jax.ShapeDtypeStruct((count * CHUNK, depth), BF16),
            jax.ShapeDtypeStruct((count * CHUNK, depth), BF16),
            jax.ShapeDtypeStruct(weight.shape, F32),
        ],
        compiler_params=params(),
        cost_estimate=LIGHT,
        name="back_project",
    )(table, *operands)


def lane_taps(conv_taps, mirrored):
    front = STRIP // 2 - RIM
    heads = conv_taps.shape[0]
    taps = conv_taps[:, ::-1] if mirrored else conv_taps
    return jnp.pad(taps, ((0, -heads % 8), (front, 2 * STRIP - front - CONV)))


def fill_bands(taps_ref, bands, heads):
    for head in range(heads):
        row = jnp.broadcast_to(taps_ref[head : head + 1, :], (STRIP, 2 * STRIP))
        bands[head] = pltpu.roll(row, 0, 1, stride=1, stride_axis=0)


def band_product(band, same, window):
    band = jnp.where(same, band, 0.0)
    high = band.astype(BF16)
    low = (band - high.astype(F32)).astype(BF16)
    return nn(high, window) + nn(low, window)


def fill_extended(kept, edge, centre_ref, rim_ref):
    rows = centre_ref.shape[0]
    kept[...] = jnp.zeros_like(kept)
    kept[edge : edge + rows, :] = centre_ref[...]
    if rim_ref is not None:
        kept[edge - RIM : edge, :] = rim_ref[:RIM, :]
        kept[edge + rows : edge + rows + RIM, :] = rim_ref[RIM:, :]


def mix_kernel(head_dim, g_ref, col_ref, v_ref, rim_ref, row_ref, taps_ref, out_ref, bands, kept):
    heads = g_ref.shape[0] // head_dim
    step = pl.program_id(0)

    @pl.when(step == 0)
    def _():
        fill_bands(taps_ref, bands, heads)
        fill_extended(kept, STRIP, v_ref, rim_ref)

    masks = head_masks(head_dim)
    window = kept[pl.ds(pl.multiple_of(step * STRIP + STRIP // 2, STRIP // 2), 2 * STRIP), :]
    ids = col_ref[...]
    same = jnp.concatenate([ids, ids], axis=1) == row_ref[pl.ds(step, 1), :]
    pieces = []
    for pair in range(heads // 2):
        values = window[:, pair * PAIR : (pair + 1) * PAIR]
        total = None
        for index, mask in enumerate(masks):
            term = band_product(bands[2 * pair + index], same, values * mask)
            total = term if total is None else total + term
        pieces.append(total)
    gathered = g_ref[...].T
    scale = lax.rsqrt(head_sum(gathered * gathered, head_dim) * (1.0 / head_dim) + EPS_UNIT)
    out_ref[...] = (gathered * scale + jnp.concatenate(pieces, axis=1)).astype(BF16)


def mix(gathered, values, rim, row, col, conv_taps, head_dim):
    width, tokens = gathered.shape
    heads = width // head_dim
    strips = tokens // STRIP
    taps = lane_taps(conv_taps, False)
    row_spec = pl.BlockSpec((STRIP, width), lambda i: (i, 0))
    whole = [values, rim, row, taps]
    return pl.pallas_call(
        partial(mix_kernel, head_dim),
        grid=(strips,),
        in_specs=[
            pl.BlockSpec((width, STRIP), lambda i: (0, i)),
            pl.BlockSpec((STRIP, PAIR), lambda i: (i + 2, 0)),
        ]
        + [pl.BlockSpec(a.shape, lambda i: (0, 0)) for a in whole],
        out_specs=row_spec,
        out_shape=jax.ShapeDtypeStruct((tokens, width), BF16),
        scratch_shapes=[
            pltpu.VMEM((heads, STRIP, 2 * STRIP), F32),
            pltpu.VMEM((tokens + 2 * STRIP, width), BF16),
        ],
        compiler_params=params(),
        cost_estimate=LIGHT,
        name="mix",
    )(gathered, col, *whole)


def back_norm_kernel(head_dim, g_ref, m_ref, out_ref):
    gathered, grad = g_ref[...].T, m_ref[...].astype(F32)
    scale = lax.rsqrt(head_sum(gathered * gathered, head_dim) * (1.0 / head_dim) + EPS_UNIT)
    mean = head_sum(grad * gathered, head_dim) * (1.0 / head_dim)
    out_ref[...] = (scale * (grad - (scale * scale) * gathered * mean)).astype(BF16)


def back_norm(gathered, grad_mixed, head_dim):
    width, tokens = gathered.shape
    row_spec = pl.BlockSpec((CHUNK, width), lambda i: (i, 0))
    return pl.pallas_call(
        partial(back_norm_kernel, head_dim),
        grid=(tokens // CHUNK,),
        in_specs=[pl.BlockSpec((width, CHUNK), lambda i: (0, i)), row_spec],
        out_specs=row_spec,
        out_shape=jax.ShapeDtypeStruct((tokens, width), BF16),
        compiler_params=params(),
        cost_estimate=LIGHT,
        name="back_norm",
    )(gathered, grad_mixed)


def back_conv_kernel(
    head_dim, col_ref, v_ref, rim_ref, m_ref, row_ref, taps_ref, dv_ref, tap_ref, bands, sums, kept_v, kept_m
):
    heads = dv_ref.shape[1] // head_dim
    step, steps = pl.program_id(0), pl.num_programs(0)

    @pl.when(step == 0)
    def _():
        fill_bands(taps_ref, bands, heads)
        fill_extended(kept_v, 2 * STRIP, v_ref, rim_ref)
        fill_extended(kept_m, 2 * STRIP, m_ref, None)
        sums[...] = jnp.zeros_like(sums)

    masks = head_masks(head_dim)
    around = pl.ds(pl.multiple_of(step * STRIP + STRIP // 2, STRIP // 2), 2 * STRIP)
    centre = pl.ds(pl.multiple_of(step * STRIP + STRIP, STRIP), STRIP)
    ids = col_ref[...]
    same = jnp.concatenate([ids, ids], axis=1) == row_ref[pl.ds(step, 1), :]
    pieces = []
    for pair in range(heads // 2):
        cols = slice(pair * PAIR, (pair + 1) * PAIR)
        grads, values, here = kept_m[around, cols], kept_v[around, cols], kept_m[centre, cols]
        total = None
        for index, mask in enumerate(masks):
            head = 2 * pair + index
            term = band_product(bands[head], same, grads * mask)
            total = term if total is None else total + term
            sums[head] += jnp.where(same, nt(here * mask, values), 0.0)
        pieces.append(total)
    dv_ref[...] = jnp.concatenate(pieces, axis=1)

    @pl.when(step == steps - 1)
    def _():
        tap_ref[...] = jnp.zeros_like(tap_ref)
        places = [lax.broadcasted_iota(jnp.int32, (STRIP, STRIP), d) for d in (0, 1)]
        flip = (places[0] + places[1] == STRIP - 1).astype(F32).astype(BF16)
        for head in range(heads):
            total = sums[head]
            high = total.astype(BF16)
            low = (total - high.astype(F32)).astype(BF16)
            turned = pltpu.roll(
                nn(flip, high) + nn(flip, low), STRIP + 1, 1, stride=1, stride_axis=0
            )
            tap_ref[head : head + 1, :] = jnp.sum(turned, axis=0, keepdims=True)


def back_conv(values, rim, grad_mixed, row, col, conv_taps, head_dim):
    tokens, width = values.shape
    heads = width // head_dim
    strips = tokens // STRIP + 2
    taps = lane_taps(conv_taps, True)
    front = STRIP // 2 - RIM
    whole = [values, rim, grad_mixed, row, taps]
    grad_values, tap_sums = pl.pallas_call(
        partial(back_conv_kernel, head_dim),
        grid=(strips,),
        in_specs=[pl.BlockSpec((STRIP, PAIR), lambda i: (i + 1, 0))]
        + [pl.BlockSpec(a.shape, lambda i: (0, 0)) for a in whole],
        out_specs=[
            pl.BlockSpec((STRIP, width), lambda i: (i, 0)),
            pl.BlockSpec(taps.shape, lambda i: (0, 0)),
        ],
        out_shape=[
            jax.ShapeDtypeStruct((strips * STRIP, width), F32),
            jax.ShapeDtypeStruct(taps.shape, F32),
        ],
        scratch_shapes=[
            pltpu.VMEM((heads, STRIP, 2 * STRIP), F32),
            pltpu.VMEM((heads, STRIP, 2 * STRIP), F32),
            pltpu.VMEM((tokens + 4 * STRIP, width), BF16),
            pltpu.VMEM((tokens + 4 * STRIP, width), BF16),
        ],
        compiler_params=params(),
        cost_estimate=LIGHT,
        name="back_conv",
    )(col, *whole)
    return grad_values, tap_sums[:heads, front : front + CONV]


def occupancy_kernel(hashes, k_ref, w_ref, out_ref, counts):
    combos = 4
    lanes = hashes * combos
    side = combos * combos
    wide = hashes * side

    @pl.when(pl.program_id(1) == 0)
    def _():
        counts[...] = jnp.zeros_like(counts)

    source = lax.broadcasted_iota(jnp.int32, (lanes, wide), 0)
    target = lax.broadcasted_iota(jnp.int32, (lanes, wide), 1)
    same_hash = (source // combos) == (target // side)
    picks = []
    for divisor in (1, combos):
        chosen = same_hash & ((source % combos) == ((target // divisor) % combos))
        picks.append(chosen.astype(F32).astype(BF16))
    keys = k_ref[...]
    for index in range(2):
        signed = nn(keys, w_ref[index])
        halves = []
        for half in range(2):
            product = None
            for pick in range(2):
                start = (half * 2 + pick) * 2 * lanes
                one = 1.0 + jnp.exp(-signed[:, start : start + lanes])
                two = 1.0 + jnp.exp(-signed[:, start + lanes : start + 2 * lanes])
                spread = nn((1.0 / (one * two)).astype(BF16), picks[pick])
                product = spread if product is None else product * spread
            halves.append(product.astype(BF16))
        low, high = halves
        for start in range(0, wide, PAIR):
            block = slice(start, start + PAIR)
            counts[index, block, :] += tn(high[:, block], low[:, block])

    @pl.when(pl.program_id(1) == pl.num_programs(1) - 1)
    def _():
        row = lax.broadcasted_iota(jnp.int32, (wide, PAIR), 0)
        lane = lax.broadcasted_iota(jnp.int32, (wide, PAIR), 1)
        diagonal = ((row % PAIR) // side) == (lane // side)
        fold = [lax.broadcasted_iota(jnp.int32, (PAIR, side * side), d) for d in (0, 1)]
        fold = ((fold[0] % side) == (fold[1] % side)).astype(F32).astype(BF16)
        spot = [lax.broadcasted_iota(jnp.int32, (wide, side * side), d) for d in (0, 1)]
        kept = (spot[0] % side) == (spot[1] // side)
        home = [lax.broadcasted_iota(jnp.int32, (hashes, wide), d) for d in (0, 1)]
        home = (home[0] == home[1] // side).astype(F32).astype(BF16)
        for index in range(2):
            left = jnp.where(diagonal, counts[index], 0.0)
            total = None
            for _ in range(3):
                piece = left.astype(BF16)
                left = left - piece.astype(F32)
                spread = jnp.where(kept, nn(piece, fold), 0.0).astype(BF16)
                term = nn(home, spread)
                total = term if total is None else total + term
            out_ref[index] = total


def occupancy(key_unit, hyperplanes, scale):
    tokens, width = key_unit.shape
    hashes, bits, head_dim = hyperplanes.shape
    pairs = width // PAIR
    wide = hashes * 16
    planes = SHARP * hyperplanes.astype(F32)
    columns = []
    for group in range(bits // 2):
        for bit in range(2):
            signs = 2.0 * ((jnp.arange(4) // (2**bit)) % 2).astype(F32) - 1.0
            plane = planes[:, 2 * group + bit, :]
            columns.append((plane.T[:, :, None] * signs).reshape(head_dim, hashes * 4))
    weight = jnp.concatenate(columns, axis=1).astype(BF16)
    blank = jnp.zeros_like(weight)
    weights = jnp.stack(
        [jnp.concatenate([weight, blank], axis=0), jnp.concatenate([blank, weight], axis=0)]
    )
    counts = pl.pallas_call(
        partial(occupancy_kernel, hashes),
        grid=(pairs, tokens // CHUNK),
        in_specs=[
            pl.BlockSpec((CHUNK, PAIR), lambda p, t: (t, p)),
            pl.BlockSpec(weights.shape, lambda p, t: (0, 0, 0)),
        ],
        out_specs=pl.BlockSpec((2, hashes, 256), lambda p, t: (p, 0, 0)),
        out_shape=jax.ShapeDtypeStruct((2 * pairs, hashes, 256), F32),
        scratch_shapes=[pltpu.VMEM((2, wide, PAIR), F32)],
        compiler_params=params(),
        cost_estimate=pl.CostEstimate(
            flops=tokens * width * 32000, bytes_accessed=tokens * width * 4, transcendentals=0
        ),
        name="occupancy",
    )(key_unit, weights)
    return counts * scale


BELL_STEP = 0.3275911
BELL = (0.254829592, -0.284496736, 1.421413741, -1.453152027, 1.061405429)


def feed_kernel(x_ref, up_ref, down_ref, out_ref, active_ref, slope_ref):
    hidden = nn(x_ref[...], up_ref[...])
    size = jnp.abs(hidden)
    step = 1.0 / (1.0 + (BELL_STEP / math.sqrt(2.0)) * size)
    poly = BELL[4]
    for factor in BELL[3::-1]:
        poly = poly * step + factor
    bell = jnp.exp(-0.5 * (hidden * hidden))
    tail = (0.5 * step) * (poly * bell)
    phi = jnp.where(hidden < 0.0, tail, 1.0 - tail)
    active = (hidden * phi).astype(BF16)
    active_ref[...] = active
    slope_ref[...] = (phi + hidden * (bell * (1.0 / math.sqrt(2.0 * math.pi)))).astype(BF16)
    out_ref[...] = nn(active, down_ref[...]).astype(BF16)


def feed(x, up_weight, down_weight):
    tokens, depth = x.shape
    hidden = up_weight.shape[1]
    rows = 256
    wide = pl.BlockSpec((rows, hidden), lambda i: (i, 0))
    narrow = pl.BlockSpec((rows, depth), lambda i: (i, 0))
    return pl.pallas_call(
        feed_kernel,
        grid=(tokens // rows,),
        in_specs=[
            narrow,
            pl.BlockSpec(up_weight.shape, lambda i: (0, 0)),
            pl.BlockSpec(down_weight.shape, lambda i: (0, 0)),
        ],
        out_specs=[narrow, wide, wide],
        out_shape=[
            jax.ShapeDtypeStruct((tokens, depth), BF16),
            jax.ShapeDtypeStruct((tokens, hidden), BF16),
            jax.ShapeDtypeStruct((tokens, hidden), BF16),
        ],
        compiler_params=params(),
        cost_estimate=LIGHT,
        name="feed",
    )(x, up_weight, down_weight)


PLANE = 4


def sum_plan(n, rows):
    unit = 16 * n
    units = -(-rows // unit)
    first = -(-2 * units // 3)
    streams = [(0, first * unit, True)]
    if units > first:
        streams.append((first * unit, (units - first) * unit, False))
    return units * unit, streams


def sum_kernel(n, streams, split, *refs):
    count = len(streams)
    table_ref, misc_ref = refs[:2]
    outs, misc_out = refs[2 : 2 + split], refs[2 + split]
    scratch = refs[3 + split :]
    send, recv = scratch[-2:]
    me = lax.axis_index("seq")
    groups = n // PLANE
    near_me, far_me = lax.rem(me, PLANE), me // PLANE

    def device(plane_first, one, two):
        return {"seq": two * PLANE + one if plane_first else one * PLANE + two}

    barrier = pltpu.get_barrier_semaphore()
    for step in range(1, PLANE):
        pl.semaphore_signal(
            barrier, 1, device_id=device(True, lax.rem(near_me + step, PLANE), far_me)
        )
    for step in range(1, groups):
        pl.semaphore_signal(
            barrier, 1, device_id=device(True, near_me, lax.rem(far_me + step, groups))
        )
    pl.semaphore_wait(barrier, PLANE - 1 + groups - 1)

    facts = []
    for index, (base, rows, plane_first) in enumerate(streams):
        sizes = (PLANE, groups) if plane_first else (groups, PLANE)
        mine = (near_me, far_me) if plane_first else (far_me, near_me)
        buffers = scratch[5 * index : 5 * index + 5]
        source = misc_ref if index == count - 1 else table_ref
        block, chunk = rows // sizes[0], rows // n
        facts.append((index, source, base, plane_first, sizes, mine, block, chunk, buffers))

    def at(start, number):
        return pl.ds(pl.multiple_of(start, 8), number)

    def start_all(phase):
        started = []
        for index, source, base, plane_first, sizes, mine, block, chunk, buffers in facts:
            got_one, part, got_two, merged, full = buffers
            side = 0 if phase in (0, 3) else 1
            for step in range(1, sizes[side]):
                to = lax.rem(mine[side] + step, sizes[side])
                if phase == 0:
                    src, dst = source.at[at(base + to * block, block), :], got_one.at[step - 1]
                elif phase == 1:
                    src, dst = part.at[at(to * chunk, chunk), :], got_two.at[step - 1]
                elif phase == 2:
                    src = dst = merged.at[at(mine[1] * chunk, chunk), :]
                else:
                    src, dst = merged, full.at[at(mine[0] * block, block), :]
                pair = (to, mine[1]) if side == 0 else (mine[0], to)
                copy = pltpu.make_async_remote_copy(
                    src_ref=src,
                    dst_ref=dst,
                    send_sem=send.at[index, phase, step - 1],
                    recv_sem=recv.at[index, phase, step - 1],
                    device_id=device(plane_first, *pair),
                    device_id_type=pl.DeviceIdType.MESH,
                )
                copy.start()
                started.append(copy)
        return started

    def wait_all(started):
        for copy in started:
            copy.wait()

    wait_all(start_all(0))
    for index, source, base, plane_first, sizes, mine, block, chunk, buffers in facts:
        got_one, part, got_two, merged, full = buffers

        def add(piece, carry):
            rows = at(piece * chunk, chunk)
            total = source[at(base + mine[0] * block + piece * chunk, chunk), :].astype(F32)
            for step in range(sizes[0] - 1):
                total = total + got_one[step, rows, :].astype(F32)
            part[rows, :] = total.astype(part.dtype)
            return carry

        lax.fori_loop(0, sizes[1], add, 0)
    wait_all(start_all(1))
    for index, source, base, plane_first, sizes, mine, block, chunk, buffers in facts:
        got_one, part, got_two, merged, full = buffers
        rows = at(mine[1] * chunk, chunk)
        total = part[rows, :].astype(F32)
        for step in range(sizes[1] - 1):
            total = total + got_two[step].astype(F32)
        merged[rows, :] = total.astype(merged.dtype)
    wait_all(start_all(2))
    started = start_all(3)
    for index, source, base, plane_first, sizes, mine, block, chunk, buffers in facts:
        merged, full = buffers[3:]
        full[at(mine[0] * block, block), :] = merged[...]
    wait_all(started)
    for index, source, base, plane_first, sizes, mine, block, chunk, buffers in facts:
        full = buffers[4]

        def put(piece, carry):
            rows = at(piece * chunk, chunk)
            if index == count - 1:
                misc_out[rows, :] = full[rows, :]
            else:
                there = at(base + piece * chunk, chunk)
                for part_index, out in enumerate(outs):
                    width = out.shape[1]
                    lanes = slice(part_index * width, (part_index + 1) * width)
                    out[there, :] = full[rows, lanes].astype(F32)
            return carry

        lax.fori_loop(0, n, put, 0)


def sum_over_seq(table, misc, split):
    n = lax.axis_size("seq")
    rows, width = table.shape
    padded, streams = sum_plan(n, rows)
    if padded > rows:
        table = jnp.pad(table, ((0, padded - rows), (0, 0)))
    lanes = -(-misc.size // (8 * n * PAIR)) * PAIR
    misc_table = jnp.pad(misc, (0, 8 * n * lanes - misc.size)).reshape(8 * n, lanes)
    streams = streams + [(0, 8 * n, True)]
    scratch = []
    for index, (_, stream_rows, plane_first) in enumerate(streams):
        last = index == len(streams) - 1
        kind, lane_count = (F32, lanes) if last else (BF16, width)
        one, two = (PLANE, n // PLANE) if plane_first else (n // PLANE, PLANE)
        block, chunk = stream_rows // one, stream_rows // n
        scratch += [
            pltpu.VMEM((one - 1, block, lane_count), kind),
            pltpu.VMEM((block, lane_count), kind),
            pltpu.VMEM((two - 1, chunk, lane_count), kind),
            pltpu.VMEM((block, lane_count), kind),
            pltpu.VMEM((stream_rows, lane_count), kind),
        ]
    partners = max(PLANE, n // PLANE) - 1
    sems = pltpu.SemaphoreType.DMA((len(streams), 4, partners))
    in_vmem = pl.BlockSpec(memory_space=pltpu.VMEM)
    shapes = [jax.ShapeDtypeStruct((padded, width // split), F32)] * split
    *sums, misc_sum = pl.pallas_call(
        partial(sum_kernel, n, streams, split),
        in_specs=[in_vmem, in_vmem],
        out_specs=[in_vmem] * (split + 1),
        out_shape=shapes + [jax.ShapeDtypeStruct(misc_table.shape, F32)],
        scratch_shapes=scratch + [sems, sems],
        compiler_params=params(collective_id=0, has_side_effects=True),
        cost_estimate=pl.CostEstimate(flops=1 << 36, bytes_accessed=1 << 24, transcendentals=0),
        name="sum_over_seq",
    )(table, misc_table)
    return [total[:rows] for total in sums], misc_sum.reshape(-1)[: misc.size]


def plan_kernel(tokens, groups, length_ref, *refs):
    outs, end_ref = refs[:-1], refs[-1]
    docs = length_ref.shape[0]
    my_index, my_side = lax.axis_index("seq"), lax.axis_index("tp")
    all_tokens = tokens * lax.axis_size("seq")
    first = my_index * tokens
    half = tokens // CHUNK

    def add(doc, total):
        total = total + length_ref[doc]
        end_ref[doc] = total
        return total

    lax.fori_loop(0, docs, add, jnp.int32(0))

    q_count = tokens // Q_TILE_BACK
    spots = [first + i * Q_TILE_BACK for i in range(q_count)]
    spots += [spot + Q_TILE_BACK - 1 for spot in spots]
    starts = []
    for distances in groups:
        starts.append([first - d * tokens + h * CHUNK for d in distances for h in range(half)])
        spots += starts[-1] + [start + CHUNK - 1 for start in starts[-1]]

    def count_ends(doc, found):
        end = end_ref[doc]
        return [f + (end <= spot).astype(jnp.int32) for f, spot in zip(found, spots)]

    found = lax.fori_loop(0, docs, count_ends, [jnp.int32(0)] * len(spots))
    found = [
        jnp.where(spot < 0, -1, jnp.where(spot >= all_tokens, FAR_ID, f))
        for f, spot in zip(found, spots)
    ]
    q_low, q_high = found[:q_count], found[q_count : 2 * q_count]
    ratio = Q_TILE // Q_TILE_BACK
    at, rest = 2 * q_count, list(outs)
    for group in starts:
        number = len(group)
        low, high = found[at : at + number], found[at + number : at + 2 * number]
        at += 2 * number
        need = [
            ((h >= q_low[0]) & (l <= q_high[-1])).astype(jnp.int32) for l, h in zip(low, high)
        ]
        ends = [
            [*q_low[::ratio], *q_high[ratio - 1 :: ratio], *low, *high],
            [*q_low, *q_high, *low, *high],
        ]
        for values in ends:
            table = rest.pop(0)
            for i, value in enumerate(values):
                table[i] = value
            base, last, taken = len(values), jnp.int32(0), jnp.int32(0)
            for i in range(number):
                table[base + i] = jnp.int32(0)
            for i in range(number):
                spot = jnp.where(need[i] > 0, taken, number - 1)
                kept = table[base + spot]
                table[base + spot] = jnp.where(need[i] > 0, i, kept)
                last = jnp.where(need[i] > 0, i, last)
                taken = taken + need[i]
            for i in range(number):
                table[base + i] = jnp.where(i < taken, table[base + i], last)
            table[base + number] = taken
        chunk_table, fill_table = rest.pop(0), rest.pop(0)
        for i in range(number):
            block, side = i % (number // 2), i // (number // 2)
            place = 2 * block + jnp.where(my_side == 0, side, 1 - side)
            one, two = need[2 * block + side], need[2 * block + 1 - side]
            wanted = jnp.where(my_side == 0, one, two)
            chunk_table[i] = place
            chunk_table[number + i] = wanted
            chunk_table[2 * number + i] = place * wanted
            fill_table[i] = jnp.where(wanted > 0, place, number)
            fill_table[number + i] = wanted
        need_ref = rest.pop(0)
        for i in range(number):
            need_ref[i] = need[i]

    def ids_of(positions):
        def step(doc, total):
            return total + (end_ref[doc] <= positions).astype(jnp.int32)

        total = lax.fori_loop(0, docs, step, jnp.zeros_like(positions))
        total = jnp.where(positions < 0, -1, total)
        return jnp.where(positions >= all_tokens, FAR_ID, total)

    def rows_of(bases, lanes):
        row = lax.broadcasted_iota(jnp.int32, (len(bases), lanes), 0)
        positions = lax.broadcasted_iota(jnp.int32, (len(bases), lanes), 1)
        for i, base in enumerate(bases):
            positions = positions + jnp.where(row == i, base, 0)
        return ids_of(positions)

    for group in starts:
        rest.pop(0)[...] = rows_of(group, CHUNK)
    rest.pop(0)[...] = rows_of([first + i * Q_TILE for i in range(tokens // Q_TILE)], Q_TILE)
    strips = tokens // STRIP
    for extra in (0, 1):
        bases = [first + i * STRIP - STRIP // 2 for i in range(-extra, strips + extra)]
        rest.pop(0)[...] = rows_of(bases, 2 * STRIP)
    col_ref = rest.pop(0)

    def fill(strip, carry):
        row = lax.broadcasted_iota(jnp.int32, (STRIP, PAIR), 0)
        rows = pl.ds(pl.multiple_of(strip * STRIP, STRIP), STRIP)
        col_ref[rows, :] = ids_of(row + (first + (strip - 2) * STRIP))
        return carry

    lax.fori_loop(0, strips + 4, fill, 0)


def plan(lengths, tokens, groups):
    half = tokens // CHUNK
    q_tiles, q_back = tokens // Q_TILE, tokens // Q_TILE_BACK
    strips = tokens // STRIP
    sizes, rows = [], []
    for distances in groups:
        number = half * len(distances)
        sizes += [
            2 * q_tiles + 3 * number + 1,
            2 * q_back + 3 * number + 1,
            3 * number,
            2 * number,
            number,
        ]
        rows.append((number, CHUNK))
    rows += [(q_tiles, Q_TILE), (strips, 2 * STRIP), (strips + 2, 2 * STRIP)]
    rows.append(((strips + 4) * STRIP, PAIR))
    smem = pl.BlockSpec(memory_space=pltpu.SMEM)
    vmem = pl.BlockSpec(memory_space=pltpu.VMEM)
    shapes = [(size,) for size in sizes] + rows
    outs = pl.pallas_call(
        partial(plan_kernel, tokens, groups),
        in_specs=[smem],
        out_specs=[smem] * len(sizes) + [vmem] * len(rows),
        out_shape=[jax.ShapeDtypeStruct(shape, jnp.int32) for shape in shapes],
        scratch_shapes=[pltpu.SMEM(lengths.shape, jnp.int32)],
        compiler_params=params(),
        cost_estimate=LIGHT,
        name="plan",
    )(lengths)
    tables = [outs[5 * i : 5 * i + 5] for i in range(len(groups))]
    return [list(column) for column in zip(*tables)], outs[len(sizes) :]


def shifted(block, axis, distance):
    count = lax.axis_size(axis)
    route = [(i, i + distance) for i in range(count) if 0 <= i + distance < count]
    return lax.ppermute(block, axis, route)


def swapped(block, axis):
    return lax.ppermute(block, axis, [(0, 1), (1, 0)])


def tp_sum(partial_low):
    return partial_low.astype(F32) + swapped(partial_low, "tp").astype(F32)


def after(value, *others):
    return lax.optimization_barrier((value, *others))[0]


def layer_norm(vectors, gain_row, shift_row):
    center = vectors - jnp.mean(vectors, axis=-1, keepdims=True)
    spread = jnp.mean(center * center, axis=-1, keepdims=True)
    return center * lax.rsqrt(spread + EPS_LAYER) * gain_row + shift_row


def body(
    inputs,
    cotangent,
    query_weight,
    key_weight,
    value_weight,
    out_weight,
    up_weight,
    down_weight,
    conv_taps,
    attn_gain,
    attn_shift,
    ffn_gain,
    ffn_shift,
    hyperplanes,
    lengths,
):
    tokens, depth = inputs.shape
    head_dim = hyperplanes.shape[2]
    width = query_weight.shape[1]
    half = tokens // 2
    my_side = lax.axis_index("tp")
    all_tokens = tokens * lax.axis_size("seq")
    far_reach = (MOST + tokens - 2) // tokens
    close = far_reach // 2
    near = list(range(close, 0, -1)) + list(range(-1, -close - 1, -1))
    far = list(range(far_reach, close, -1)) + list(range(-close - 1, -far_reach - 1, -1))

    mine_rows = lax.dynamic_slice_in_dim(inputs, my_side * half, half, 0)
    near_mine = [shifted(mine_rows, "seq", d) for d in near]

    near_at, far_at, own_at = range(3)
    k_counts = [tokens // CHUNK * len(distances) for distances in (near, far, [0])]
    (tables, back_tables, chunk_tables, fill_tables, needs), id_rows = plan(
        lengths, tokens, (near, far, [0])
    )
    near_rows, far_rows, own_key_rows, own_rows, mix_row, back_row, ids_col = id_rows

    weight_qkv = jnp.concatenate([query_weight, key_weight, value_weight], axis=1)
    weight_kv = weight_qkv[:, width:]
    plain_table = jnp.array(list(range(tokens // CHUNK)) + [1] * (tokens // CHUNK), jnp.int32)
    query_unit, query_scale, key_unit, key_scale, values = project(
        plain_table, [inputs], weight_qkv, 2, head_dim
    )
    gathered, own_weights = attend(
        tables[own_at], query_unit, key_unit, values, own_rows, own_key_rows, head_dim
    )

    def other_half(mine):
        return jnp.concatenate([swapped(term, "tp") for term in mine], axis=0)

    *near_mine, late_rows = after((*near_mine, mine_rows), gathered)
    far_mine = [shifted(late_rows if i else mine_rows, "seq", d) for i, d in enumerate(far)]
    group_x, group_kv, group_weights = [], [], []
    for index, mine in ((near_at, near_mine), (far_at, far_mine)):
        if index == far_at:
            mine = after(tuple(mine), gathered)
        group_x.append([*mine, other_half(mine)])
        key_far, scale_far, value_far = project(
            fill_tables[index], group_x[index], weight_kv, 1, head_dim, k_counts[index]
        )
        group_kv.append((key_far, scale_far, value_far))
        gathered, weights = attend(
            tables[index],
            query_unit,
            key_far,
            value_far,
            own_rows,
            (near_rows, far_rows)[index],
            head_dim,
            seed=gathered,
        )
        group_weights.append(weights)
    edge = close * tokens
    sides = needs[near_at][edge // CHUNK - 1 : edge // CHUNK + 1]
    values_rim = jnp.where(
        jnp.repeat(sides, RIM)[:, None] > 0, group_kv[near_at][2][edge - RIM : edge + RIM], 0
    )
    mixed = mix(gathered, values, values_rim, mix_row, ids_col, conv_taps, head_dim)

    attn_out = tp_sum(nn(mixed, out_weight).astype(BF16))
    first_norm, first_back = jax.vjp(
        layer_norm, inputs.astype(F32) + attn_out, attn_gain, attn_shift
    )
    first_low = first_norm.astype(BF16)
    partial_out, active, slope = feed(first_low, up_weight, down_weight)
    ffn_out = tp_sum(partial_out)
    result, second_back = jax.vjp(layer_norm, first_norm + ffn_out, ffn_gain, ffn_shift)
    output = result.astype(BF16)
    grad_second, grad_ffn_gain, grad_ffn_shift = second_back(cotangent.astype(F32))
    grad_ffn = grad_second.astype(BF16)
    grad_hidden = (nt(grad_ffn, down_weight) * slope.astype(F32)).astype(BF16)
    grad_first = grad_second + tp_sum(nt(grad_hidden, up_weight).astype(BF16))
    grad_residual, grad_attn_gain, grad_attn_shift = first_back(grad_first)
    grad_attn = grad_residual.astype(BF16)
    grad_mixed = nt(grad_attn, out_weight).astype(BF16)

    grad_down = tn(active, grad_ffn).astype(BF16)
    grad_up = tn(first_low, grad_hidden).astype(BF16)
    grad_out = tn(mixed, grad_attn).astype(BF16)
    down_out = jnp.concatenate([grad_down, grad_out], axis=0)
    grad_up_low, down_out_low = grad_up, down_out
    grad_up, down_out = lax.psum((grad_up_low, down_out_low), "seq")

    grad_rows = back_norm(gathered, after(grad_mixed, grad_up_low, down_out_low), head_dim)

    def back_scores(index, grad_rows, seed):
        key_far, _, value_far = group_kv[index]
        return back_attend(
            back_tables[index],
            k_counts[index],
            query_unit,
            grad_rows,
            key_far,
            value_far,
            group_weights[index],
            head_dim,
            seed=seed,
        )

    def back_inputs(index, dk, dv, **rims):
        key_far, scale_far, _ = group_kv[index]
        parts = [(key_far, scale_far, dk)]
        return back_project(
            chunk_tables[index], group_x[index], weight_kv, parts, 0, [dv], head_dim, **rims
        )

    def send_home(distances, dx_mine, came):
        both = [
            (
                dx_mine[i * half : (i + 1) * half].astype(F32)
                + came[i * half : (i + 1) * half].astype(F32)
            ).astype(BF16)
            for i in range(len(distances))
        ]
        return both, [shifted(term, "seq", -d) for term, d in zip(both, distances)]

    dk, dv, turned = back_scores(far_at, grad_rows, None)
    far_dx, dx_other, far_dw = back_inputs(far_at, dk, dv)
    far_came = swapped(dx_other, "tp")
    grad_conv_values, grad_taps = back_conv(
        values, values_rim, after(grad_mixed, far_dx), back_row, ids_col, conv_taps, head_dim
    )
    rim = jnp.concatenate([grad_conv_values[:STRIP], grad_conv_values[-STRIP:]], axis=0)
    dk, dv, turned = back_scores(near_at, after(grad_rows, grad_conv_values), turned)
    near_dx, dx_other, near_dw = back_inputs(
        near_at, dk, dv, rims=close * (tokens // CHUNK) - 1, rim=rim
    )
    near_came = swapped(dx_other, "tp")
    far_came, grad_up, down_out = after((far_came, grad_up, down_out), near_dx)
    terms, far_homes = send_home(far, far_dx, far_came)
    dk, dv, turned = back_attend(
        back_tables[own_at],
        k_counts[own_at],
        query_unit,
        after(grad_rows, *terms),
        key_unit,
        values,
        own_weights,
        head_dim,
        seed=turned,
        cost=pl.CostEstimate(flops=1 << 35, bytes_accessed=1 << 20, transcendentals=0),
    )
    terms, near_homes = send_home(near, near_dx, after(near_came, dk))
    dk, key_late, far_homes = after((dk, key_unit, far_homes), *terms)
    own_mine = mine_rows
    own_other = lax.dynamic_slice_in_dim(inputs, (1 - my_side) * half, half, 0)
    dx_mine, dx_other, dw = back_project(
        chunk_tables[own_at],
        [own_mine, own_other],
        weight_qkv,
        [(query_unit, query_scale, turned), (key_unit, key_scale, dk)],
        1,
        [dv, grad_conv_values[STRIP:-STRIP]],
        head_dim,
    )

    occ_local = occupancy(after(key_late, dw), hyperplanes, 2.0**BITS / all_tokens)
    near_homes = after(tuple(near_homes), occ_local)
    qkv = jnp.concatenate([dw[:, :width], dw[:, width:] + near_dw + far_dw], axis=1).astype(BF16)
    misc = [
        occ_local,
        grad_taps,
        grad_attn_gain,
        grad_attn_shift,
        grad_ffn_gain,
        grad_ffn_shift,
    ]
    packed = jnp.concatenate([term.reshape(-1) for term in misc])
    qkv, packed = sum_over_seq(qkv, packed, 3)

    came = swapped(dx_other, "tp")
    total = (
        lax.dynamic_slice_in_dim(grad_residual, my_side * half, half, 0)
        + dx_mine.astype(F32)
        + came.astype(F32)
    )
    for home in (*far_homes, *near_homes):
        total = total + home.astype(F32)
    other_total = swapped(total, "tp")
    lower = jnp.where(my_side == 0, total, other_total)
    upper = jnp.where(my_side == 0, other_total, total)
    grad_inputs = jnp.concatenate([lower, upper], axis=0)

    unpacked, at = [], 0
    for term in misc:
        unpacked.append(packed[at : at + term.size].reshape(term.shape))
        at += term.size
    down_out = down_out.astype(F32)
    ff = down_weight.shape[0]
    return (
        output,
        grad_inputs,
        *qkv,
        down_out[ff:],
        grad_up.astype(F32),
        down_out[:ff],
        *unpacked[1:],
        unpacked[0],
    )


def solution(mesh):
    return jax.shard_map(
        body,
        mesh=mesh,
        in_specs=(
            P("seq", None),
            P("seq", None),
            P(None, "tp"),
            P(None, "tp"),
            P(None, "tp"),
            P("tp", None),
            P(None, "tp"),
            P("tp", None),
            P("tp", None),
            P(),
            P(),
            P(),
            P(),
            P(),
            P(),
        ),
        out_specs=(
            P("seq", None),
            P("seq", None),
            P(None, "tp"),
            P(None, "tp"),
            P(None, "tp"),
            P("tp", None),
            P(None, "tp"),
            P("tp", None),
            P("tp", None),
            P(),
            P(),
            P(),
            P(),
            P("tp", None, None),
        ),
        check_vma=False,
    )
```

profile of v0, /device:TPU:0, one launch (start us, length us, event | category | flops | bytes accessed | tf_op | source)
XLA Modules:
  0.0 698.6 jit_solution(879994490685726811)
XLA Ops:
  7.3 2.5 constant_dynamic-slice_fusion
  12.3 5.5 collective-permute-start.2
  17.9 4.6 collective-permute-start.1
  22.4 12.3 %plan.1 = (s32[29]{0:T(128)}, s32[33]{0:T(128)}, s32[24]{0:T(128)}, s32[16]{0:T(128)}, s32[8]{0:T(128)}, /*index=5*/s32[29]{0:T(128)}, s32[33]{0:T(128)}, s32[24...) custom-call(s32[32]{0:T(128)} %length_ref.1), custom_call_target="tpu_custom_call" | custom-call | flops 1048576 | bytes 65536 | tf_op jit(solution)/shard_map/plan/pallas_call | solution.py:1093
  37.4 7.4 %project.3 = (bf16[1024,384]{1,0:T(8,128)(2,1)}, f32[1024,384]{1,0:T(8,128)}, bf16[1024,384]{1,0:T(8,128)(2,1)}, f32[1024,384]{1,0:T(8,128)}, bf16[1024,384]{1,0:T(8,128)(2,1)}) custom-call(s32[4]{0:T(128)} %constant.115.clone.table, bf16[1024,768]{1,0:T(8,128)(2,1)} %refs_0_.1, bf16[768,1152]{1,0:T(8,128)(2,1)} %copy-done.11), custom_call_target="tpu_custom_call" | custom-call | flops 3623878656 | bytes 786432 | tf_op jit(solution)/shard_map/project/pallas_call | solution.py:138
  44.8 31.5 %attend.3 = (f32[384,1024]{1,0:T(8,128)}, bf16[6,1024,1024]{2,1,0:T(8,128)(2,1)}) custom-call(s32[11]{0:T(128)} %get-tuple-element.110.table, bf16[1024,384]{1,0:T(8,128)(2,1)} %get-tuple-element.106.q_ref.refs_3_, s32[2,512]{1,0:T(2,128)} %get-tuple-element.107.qrow_ref, s32[2,512]{1,0:T(2,128)} %get-tuple-element.111.krow_ref, ...), custom_call_target="tpu_custom_call" | custom-call | flops 12884901888 | bytes 1572864 | tf_op jit(solution)/shard_map/attend/pallas_call | solution.py:252
  77.4 3.2 collective-permute-start
  83.3 7.6 %collective-permute-start.5 = (bf16[512,768]{1,0:T(8,128)(2,1)S(1)}, bf16[512,768]{1,0:T(8,128)(2,1)}, u32[]{:S(2)}, u32[]{:S(2)}) collective-permute-start(bf16[512,768]{1,0:T(8,128)(2,1)S(1)} %get-tuple-element.115.refs_0_), channel_id=1, source_target_pairs={{0,6},{2,8},{4,10},{6,12},{8,14},{10,16},{12,18},{14,20},{16,22},{... | collective-permute-start | bytes 2359304 | tf_op jit(solution)/shard_map/ppermute | solution.py:1110
  92.8 9.4 %project.4 = (bf16[4608,384]{1,0:T(8,128)(2,1)}, f32[4608,384]{1,0:T(8,128)}, bf16[4608,384]{1,0:T(8,128)(2,1)}) custom-call(s32[16]{0:T(128)} %get-tuple-element.118.table, bf16[512,768]{1,0:T(8,128)(2,1)} %copy-done.25, bf16[512,768]{1,0:T(8,128)(2,1)} %copy-done.24, bf16[512,768]{1,0:T(8,128)(2,1)} %copy-done.23, bf16[512,768]{1,0:T(8,128)(2,1)} %copy-done.22, ...), custom_call_target="tpu_custom_call" | custom-call | flops 9663676416 | bytes 3145728 | tf_op jit(solution)/shard_map/project/pallas_call | solution.py:138
  102.2 16.8 %attend.4 = (f32[384,1024]{1,0:T(8,128)}, bf16[6,4096,1024]{2,1,0:T(8,128)(2,1)}) custom-call(s32[29]{0:T(128)} %get-tuple-element.116.table, bf16[1024,384]{1,0:T(8,128)(2,1)} %get-tuple-element.106.q_ref.refs_3_, s32[2,512]{1,0:T(2,128)} %get-tuple-element.107.qrow_ref, s32[8,512]{1,0:T(8,128)} %get-tuple-element.117.krow_ref, ...), custom_call_target="tpu_custom_call" | custom-call | flops 51539607552 | bytes 1572864 | tf_op jit(solution)/shard_map/attend/pallas_call | solution.py:252
  119.0 4.4 collective-permute-done.5.refs_1_
  131.0 7.4 %project.5 = (bf16[4608,384]{1,0:T(8,128)(2,1)}, f32[4608,384]{1,0:T(8,128)}, bf16[4608,384]{1,0:T(8,128)(2,1)}) custom-call(s32[16]{0:T(128)} %get-tuple-element.109.table, bf16[512,768]{1,0:T(8,128)(2,1)} %collective-permute-done.refs_0_, bf16[512,768]{1,0:T(8,128)(2,1)} %collective-permute-done.5.refs_1_, ...), custom_call_target="tpu_custom_call" | custom-call | flops 9663676416 | bytes 3145728 | tf_op jit(solution)/shard_map/project/pallas_call | solution.py:138
  138.4 9.5 %attend.5 = (f32[384,1024]{1,0:T(8,128)}, bf16[6,4096,1024]{2,1,0:T(8,128)(2,1)}) custom-call(s32[29]{0:T(128)} %get-tuple-element.105.table, bf16[1024,384]{1,0:T(8,128)(2,1)} %get-tuple-element.106.q_ref.refs_3_, s32[2,512]{1,0:T(2,128)} %get-tuple-element.107.qrow_ref, s32[8,512]{1,0:T(8,128)} %get-tuple-element.108.krow_ref, ...), custom_call_target="tpu_custom_call" | custom-call | flops 51539607552 | bytes 1572864 | tf_op jit(solution)/shard_map/attend/pallas_call | solution.py:252
  147.8 8.2 %mix.1 = bf16[1024,384]{1,0:T(8,128)(2,1)} custom-call(f32[384,1024]{1,0:T(8,128)} %get-tuple-element.132.g_ref, s32[1536,128]{1,0:T(8,128)} %get-tuple-element.133.col_ref, bf16[1024,384]{1,0:T(8,128)(2,1)} %get-tuple-element.113.v_ref, bf16[32,384]{1,0:T(8,128)(2,1)} %slice_select_fusion.rim_ref, s32[8,256]{1,0:T(8,128)} %get-tuple-element.135.row_ref, ...), custom_call_target="tpu_custom_call" | custom-call | flops 1048576 | bytes 65536 | tf_op jit(solution)/shard_map/mix/pallas_call | solution.py:537
  156.1 2.1 convolution_convert_fusion.2
  158.4 3.3 collective-permute-done.16
  164.8 12.8 %feed.1 = (bf16[1024,768]{1,0:T(8,128)(2,1)}, bf16[1024,1536]{1,0:T(8,128)(2,1)}, bf16[1024,1536]{1,0:T(8,128)(2,1)}) custom-call(bf16[1024,768]{1,0:T(8,128)(2,1)} %fusion.4.x_ref, bf16[768,1536]{1,0:T(8,128)(2,1)} %up_ref.1, bf16[1536,768]{1,0:T(8,128)(2,1)} %down_ref.1), custom_call_target="tpu_custom_call" | custom-call | flops 1048576 | bytes 65536 | tf_op jit(solution)/shard_map/feed/pallas_call | solution.py:778
  177.8 3.5 collective-permute-done.17
  181.2 2.6 fusion.18
  187.1 2.6 fusion.17
  190.2 3.0 multiply_convert_fusion
  193.2 2.6 convolution_convert_fusion.3
  196.1 4.2 convolution_convert_fusion.1
  200.2 3.3 convolution_convert_fusion
  203.5 2.1 multiply_reduce_fusion
  209.9 1.9 convolution_convert_fusion.4.m_ref
  213.6 3.6 back_norm.1.g_ref
  217.2 10.6 %back_attend.3 = (bf16[4096,384]{1,0:T(8,128)(2,1)}, bf16[4096,384]{1,0:T(8,128)(2,1)}, f32[384,1024]{1,0:T(8,128)}) custom-call(s32[33]{0:T(128)} %get-tuple-element.145.table, bf16[1024,384]{1,0:T(8,128)(2,1)} %get-tuple-element.106.q_ref.refs_3_, bf16[1024,384]{1,0:T(8,128)(2,1)} %back_norm.1.g_ref, bf16[4608,384]{1,0:T(8,128)(2,1)} %get-tuple-element.130.k_ref.refs_6_, ...), custom_call_target="tpu_custom_call" | custom-call | flops 1048576 | bytes 65536 | tf_op jit(solution)/shard_map/back_attend/pallas_call | solution.py:349
  227.8 11.1 %back_project.3 = (bf16[2048,768]{1,0:T(8,128)(2,1)}, bf16[2048,768]{1,0:T(8,128)(2,1)}, f32[768,768]{1,0:T(8,128)}) custom-call(s32[24]{0:T(128)} %get-tuple-element.143.table, bf16[512,768]{1,0:T(8,128)(2,1)} %collective-permute-done.refs_0_, bf16[512,768]{1,0:T(8,128)(2,1)} %collective-permute-done.5.refs_1_, ...), custom_call_target="tpu_custom_call" | custom-call | flops 1048576 | bytes 65536 | tf_op jit(solution)/shard_map/back_project/pallas_call | solution.py:455
  242.3 10.1 %back_conv.1 = (f32[1280,384]{1,0:T(8,128)}, f32[8,256]{1,0:T(8,128)}) custom-call(s32[1536,128]{1,0:T(8,128)} %get-tuple-element.133.col_ref, bf16[1024,384]{1,0:T(8,128)(2,1)} %get-tuple-element.113.v_ref, bf16[32,384]{1,0:T(8,128)(2,1)} %slice_select_fusion.rim_ref, bf16[1024,384]{1,0:T(8,128)(2,1)} %convolution_convert_fusion.4.m_ref, ...), custom_call_target="tpu_custom_call" | custom-call | flops 1048576 | bytes 65536 | tf_op jit(solution)/shard_map/back_conv/pallas_call | solution.py:632
  252.4 2.7 slice.154.refs_10_
  255.3 14.3 %back_attend.4 = (bf16[4096,384]{1,0:T(8,128)(2,1)}, bf16[4096,384]{1,0:T(8,128)(2,1)}, f32[384,1024]{1,0:T(8,128)}) custom-call(s32[33]{0:T(128)} %get-tuple-element.153.table, bf16[1024,384]{1,0:T(8,128)(2,1)} %get-tuple-element.106.q_ref.refs_3_, bf16[1024,384]{1,0:T(8,128)(2,1)} %back_norm.1.g_ref, bf16[4608,384]{1,0:T(8,128)(2,1)} %get-tuple-element.123.k_ref.refs_6_, ...), custom_call_target="tpu_custom_call" | custom-call | flops 1048576 | bytes 65536 | tf_op jit(solution)/shard_map/back_attend/pallas_call | solution.py:349
  271.4 14.8 %back_project.4 = (bf16[2048,768]{1,0:T(8,128)(2,1)}, bf16[2048,768]{1,0:T(8,128)(2,1)}, f32[768,768]{1,0:T(8,128)}) custom-call(s32[24]{0:T(128)} %get-tuple-element.151.table, bf16[512,768]{1,0:T(8,128)(2,1)} %copy-done.25, bf16[512,768]{1,0:T(8,128)(2,1)} %copy-done.24, bf16[512,768]{1,0:T(8,128)(2,1)} %copy-done.23, bf16[512,768]{1,0:T(8,128)(2,1)} %copy-done.22, ...), custom_call_target="tpu_custom_call" | custom-call | flops 1048576 | bytes 65536 | tf_op jit(solution)/shard_map/back_project/pallas_call | solution.py:455
  286.3 216.9 %all-reduce.8.cloned.1.call-done = (bf16[768,1536]{1,0:T(8,128)(2,1)}, bf16[1920,768]{1,0:T(8,128)(2,1)}) async-done(((bf16[768,1536]{1,0:T(8,128)(2,1)}, bf16[1920,768]{1,0:T(8,128)(2,1)}), (bf16[768,1536]{1,0:T(8,128)(2,1)}, bf16[1920,768]{1,0:T(8,128)(2,1)})) %all-reduce.8.cloned.1.call-update) | async-done | bytes 5308432 | tf_op jit(solution)/shard_map/psum | solution.py:1233
  503.2 3.5 add_convert_fusion.7
  506.7 3.4 collective-permute-start.23
  510.2 5.2 collective-permute-start.22
  518.0 26.0 %back_attend.5 = (bf16[1024,384]{1,0:T(8,128)(2,1)}, bf16[1024,384]{1,0:T(8,128)(2,1)}, f32[384,1024]{1,0:T(8,128)}) custom-call(s32[15]{0:T(128)} %get-tuple-element.140.table, bf16[1024,384]{1,0:T(8,128)(2,1)} %get-tuple-element.106.q_ref.refs_3_, bf16[1024,384]{1,0:T(8,128)(2,1)} %back_norm.1.g_ref, bf16[1024,384]{1,0:T(8,128)(2,1)} %get-tuple-element.182.k_ref.refs_6_, ...), custom_call_target="tpu_custom_call" | custom-call | flops 34359738368 | bytes 1048576 | tf_op jit(solution)/shard_map/back_attend/pallas_call | solution.py:349
  545.1 2.6 slice.185
  548.4 2.8 add_convert_fusion.3
  551.2 6.9 collective-permute-start.29
  558.1 2.8 convert_element_type.270
  561.0 5.7 collective-permute-start.28
  569.3 15.5 %back_project.5 = (bf16[512,768]{1,0:T(8,128)(2,1)}, bf16[512,768]{1,0:T(8,128)(2,1)}, f32[768,1152]{1,0:T(8,128)}) custom-call(s32[6]{0:T(128)} %get-tuple-element.138.table, bf16[512,768]{1,0:T(8,128)(2,1)} %copy-done.12, bf16[512,768]{1,0:T(8,128)(2,1)} %get-tuple-element.226.refs_1_, bf16[768,1152]{1,0:T(8,128)(2,1)} %copy-done.11, ...), custom_call_target="tpu_custom_call" | custom-call | flops 1048576 | bytes 65536 | tf_op jit(solution)/shard_map/back_project/pallas_call | solution.py:455
  584.9 19.6 %occupancy.1 = f32[6,32,256]{2,1,0:T(8,128)} custom-call(bf16[1024,384]{1,0:T(8,128)(2,1)} %get-tuple-element.182.k_ref.refs_6_, bf16[2,128,1024]{2,1,0:T(8,128)(2,1)} %pad_maximum_fusion.3.w_ref), custom_call_target="tpu_custom_call" | custom-call | flops 12582912000 | bytes 1572864 | tf_op jit(solution)/shard_map/occupancy/pallas_call | solution.py:733
  608.6 2.8 add_convert_fusion.2
  613.9 3.9 convert_add_fusion
  618.4 62.3 %sum_over_seq.1 = (f32[768,384]{1,0:T(8,128)}, f32[768,384]{1,0:T(8,128)}, f32[768,384]{1,0:T(8,128)}, f32[128,512]{1,0:T(8,128)}) custom-call(bf16[768,1152]{1,0:T(8,128)(2,1)} %pad_maximum_fusion.2.refs_0_, f32[128,512]{1,0:T(8,128)} %reshape.195.refs_1_), custom_call_target="tpu_custom_call" | custom-call | flops 68719476736 | bytes 16777216 | tf_op jit(solution)/shard_map/sum_over_seq/pallas_call | solution.py:950
  (232 shorter events, 61.7 us)
Async XLA Ops:
  7.2 148.9 %copy-start = (bf16[384,768]{1,0:T(8,128)(2,1)S(1)}, bf16[384,768]{1,0:T(8,128)(2,1)}, u32[]{:S(2)}) copy-start(bf16[384,768]{1,0:T(8,128)(2,1)} %param.21) | copy-start | bytes 1769476
  7.2 27.7 %copy-start.29 = (bf16[768,384]{1,0:T(8,128)(2,1)S(1)}, bf16[768,384]{1,0:T(8,128)(2,1)}, u32[]{:S(2)}) copy-start(bf16[768,384]{1,0:T(8,128)(2,1)} %param.19) | copy-start | bytes 1769476
  7.2 496.0 %all-reduce.8.cloned.1.call-start = ((), (), s32[]{:S(2)}) async-start(), calls=%async_computation | async-start | bytes 10616832 | tf_op jit(solution)/shard_map/psum | solution.py:1233
  7.3 27.5 %copy-start.31 = (bf16[768,384]{1,0:T(8,128)(2,1)S(1)}, bf16[768,384]{1,0:T(8,128)(2,1)}, u32[]{:S(2)}) copy-start(bf16[768,384]{1,0:T(8,128)(2,1)} %param.18) | copy-start | bytes 1769476
  9.7 73.6 %copy-start.12 = (bf16[512,768]{1,0:T(8,128)(2,1)}, bf16[512,768]{1,0:T(8,128)(2,1)S(1)}, u32[]{:S(2)}) copy-start(bf16[512,768]{1,0:T(8,128)(2,1)S(1)} %get-tuple-element.115.refs_0_) | copy-start | bytes 2359300
  9.7 66.5 %collective-permute-start.4 = (bf16[512,768]{1,0:T(8,128)(2,1)S(1)}, bf16[512,768]{1,0:T(8,128)(2,1)S(1)}, u32[]{:S(2)}, u32[]{:S(2)}) collective-permute-start(bf16[512,768]{1,0:T(8,128)(2,1)S(1)} %get-tuple-element.115.refs_0_), channel_id=1, source_target_pairs={{4,0},{6,2},{8,4},{10,6},{12,8},{14,10},{16,12},{18,14},{20,16},{2... | collective-permute-start | bytes 2359304 | tf_op jit(solution)/shard_map/ppermute | solution.py:1110
  11.0 65.2 %collective-permute-start.3 = (bf16[512,768]{1,0:T(8,128)(2,1)S(1)}, bf16[512,768]{1,0:T(8,128)(2,1)S(1)}, u32[]{:S(2)}, u32[]{:S(2)}) collective-permute-start(bf16[512,768]{1,0:T(8,128)(2,1)S(1)} %get-tuple-element.115.refs_0_), channel_id=1, source_target_pairs={{2,0},{4,2},{6,4},{8,6},{10,8},{12,10},{14,12},{16,14},{18,16},{20... | collective-permute-start | bytes 2359304 | tf_op jit(solution)/shard_map/ppermute | solution.py:1110
  12.3 64.0 %collective-permute-start.2 = (bf16[512,768]{1,0:T(8,128)(2,1)S(1)}, bf16[512,768]{1,0:T(8,128)(2,1)S(1)}, u32[]{:S(2)}, u32[]{:S(2)}) collective-permute-start(bf16[512,768]{1,0:T(8,128)(2,1)S(1)} %get-tuple-element.115.refs_0_), channel_id=1, source_target_pairs={{0,2},{2,4},{4,6},{6,8},{8,10},{10,12},{12,14},{14,16},{16,18},{18... | collective-permute-start | bytes 2359304 | tf_op jit(solution)/shard_map/ppermute | solution.py:1110
  17.9 58.5 %collective-permute-start.1 = (bf16[512,768]{1,0:T(8,128)(2,1)S(1)}, bf16[512,768]{1,0:T(8,128)(2,1)S(1)}, u32[]{:S(2)}, u32[]{:S(2)}) collective-permute-start(bf16[512,768]{1,0:T(8,128)(2,1)S(1)} %get-tuple-element.115.refs_0_), channel_id=1, source_target_pairs={{0,4},{2,6},{4,8},{6,10},{8,12},{10,14},{12,16},{14,18},{16,20},{1... | collective-permute-start | bytes 2359304 | tf_op jit(solution)/shard_map/ppermute | solution.py:1110
  76.3 14.8 %copy-start.22 = (bf16[512,768]{1,0:T(8,128)(2,1)}, bf16[512,768]{1,0:T(8,128)(2,1)S(1)}, u32[]{:S(2)}) copy-start(bf16[512,768]{1,0:T(8,128)(2,1)S(1)} %collective-permute-done.4.refs_3_) | copy-start | bytes 2359300
  76.3 14.8 %copy-start.23 = (bf16[512,768]{1,0:T(8,128)(2,1)}, bf16[512,768]{1,0:T(8,128)(2,1)S(1)}, u32[]{:S(2)}) copy-start(bf16[512,768]{1,0:T(8,128)(2,1)S(1)} %collective-permute-done.3.refs_2_) | copy-start | bytes 2359300
  76.3 14.8 %copy-start.24 = (bf16[512,768]{1,0:T(8,128)(2,1)}, bf16[512,768]{1,0:T(8,128)(2,1)S(1)}, u32[]{:S(2)}) copy-start(bf16[512,768]{1,0:T(8,128)(2,1)S(1)} %collective-permute-done.2.refs_1_) | copy-start | bytes 2359300
  76.3 14.8 %copy-start.25 = (bf16[512,768]{1,0:T(8,128)(2,1)}, bf16[512,768]{1,0:T(8,128)(2,1)S(1)}, u32[]{:S(2)}) copy-start(bf16[512,768]{1,0:T(8,128)(2,1)S(1)} %collective-permute-done.1.refs_0_) | copy-start | bytes 2359300
  76.3 4.3 collective-permute-start.8
  76.4 5.5 collective-permute-start.9
  76.9 6.4 collective-permute-start.10
  77.0 14.0 %collective-permute-start.11 = (bf16[512,768]{1,0:T(8,128)(2,1)S(1)}, bf16[512,768]{1,0:T(8,128)(2,1)S(1)}, u32[]{:S(2)}, u32[]{:S(2)}) collective-permute-start(bf16[512,768]{1,0:T(8,128)(2,1)S(1)} %collective-permute-done.4.refs_3_), channel_id=1, source_target_pairs={{0,1},{1,0},{2,3},{3,2},{4,5},{5,4},{6,7},{7,6},{8,9},{9,8},{10,11... | collective-permute-start | bytes 2359304 | tf_op jit(solution)/shard_map/ppermute | solution.py:1114
  77.4 41.6 %collective-permute-start = (bf16[512,768]{1,0:T(8,128)(2,1)S(1)}, bf16[512,768]{1,0:T(8,128)(2,1)}, u32[]{:S(2)}, u32[]{:S(2)}) collective-permute-start(bf16[512,768]{1,0:T(8,128)(2,1)S(1)} %get-tuple-element.115.refs_0_), channel_id=1, source_target_pairs={{0,8},{2,10},{4,12},{6,14},{8,16},{10,18},{12,20},{14,22},{16,24},... | collective-permute-start | bytes 2359304 | tf_op jit(solution)/shard_map/ppermute | solution.py:1110
  80.6 38.4 %collective-permute-start.7 = (bf16[512,768]{1,0:T(8,128)(2,1)S(1)}, bf16[512,768]{1,0:T(8,128)(2,1)}, u32[]{:S(2)}, u32[]{:S(2)}) collective-permute-start(bf16[512,768]{1,0:T(8,128)(2,1)S(1)} %get-tuple-element.115.refs_0_), channel_id=1, source_target_pairs={{8,0},{10,2},{12,4},{14,6},{16,8},{18,10},{20,12},{22,14},{24,16},... | collective-permute-start | bytes 2359304 | tf_op jit(solution)/shard_map/ppermute | solution.py:1110
  81.9 37.0 %collective-permute-start.6 = (bf16[512,768]{1,0:T(8,128)(2,1)S(1)}, bf16[512,768]{1,0:T(8,128)(2,1)}, u32[]{:S(2)}, u32[]{:S(2)}) collective-permute-start(bf16[512,768]{1,0:T(8,128)(2,1)S(1)} %get-tuple-element.115.refs_0_), channel_id=1, source_target_pairs={{6,0},{8,2},{10,4},{12,6},{14,8},{16,10},{18,12},{20,14},{22,16},{... | collective-permute-start | bytes 2359304 | tf_op jit(solution)/shard_map/ppermute | solution.py:1110
  83.3 40.1 %collective-permute-start.5 = (bf16[512,768]{1,0:T(8,128)(2,1)S(1)}, bf16[512,768]{1,0:T(8,128)(2,1)}, u32[]{:S(2)}, u32[]{:S(2)}) collective-permute-start(bf16[512,768]{1,0:T(8,128)(2,1)S(1)} %get-tuple-element.115.refs_0_), channel_id=1, source_target_pairs={{0,6},{2,8},{4,10},{6,12},{8,14},{10,16},{12,18},{14,20},{16,22},{... | collective-permute-start | bytes 2359304 | tf_op jit(solution)/shard_map/ppermute | solution.py:1110
  102.2 22.2 %copy-start.43 = (s32[8]{0:T(128)S(1)}, s32[8]{0:T(128)}, u32[]{:S(2)}) copy-start(s32[8]{0:T(128)} %get-tuple-element.134) | copy-start | bytes 100
  102.2 22.5 %copy-start.38 = (f32[6,33]{1,0:T(8,128)S(1)}, f32[6,33]{1,0:T(8,128)}, u32[]{:S(2)}) copy-start(f32[6,33]{1,0:T(8,128)} %param.24) | copy-start | bytes 2380
  123.4 3.7 collective-permute-start.12
  123.4 4.9 collective-permute-start.13
  123.9 4.5 collective-permute-start.14
  123.9 5.4 collective-permute-start.15
  147.8 13.8 %copy-start.6 = (bf16[1024,768]{1,0:T(8,128)(2,1)S(1)}, bf16[1024,768]{1,0:T(8,128)(2,1)}, u32[]{:S(2)}) copy-start(bf16[1024,768]{1,0:T(8,128)(2,1)} %refs_0_.1) | copy-start | bytes 4718596
  158.2 3.5 collective-permute-start.16
  177.6 3.6 collective-permute-start.17
  195.9 7.7 %collective-permute-start.18 = (bf16[1024,768]{1,0:T(8,128)(2,1)S(1)}, bf16[1024,768]{1,0:T(8,128)(2,1)S(1)}, u32[]{:S(2)}, u32[]{:S(2)}) collective-permute-start(bf16[1024,768]{1,0:T(8,128)(2,1)S(1)} %convolution_convert_fusion.3), channel_id=1, source_target_pairs={{0,1},{1,0},{2,3},{3,2},{4,5},{5,4},{6,7},{7,6},{8,9},{9,8},{10,11... | collective-permute-start | bytes 4718600 | tf_op jit(solution)/shard_map/ppermute | solution.py:1114
  227.8 12.6 %copy-start.33 = (bf16[32,8,64]{2,1,0:T(8,128)(2,1)S(1)}, bf16[32,8,64]{2,1,0:T(8,128)(2,1)}, u32[]{:S(2)}) copy-start(bf16[32,8,64]{2,1,0:T(8,128)(2,1)} %param.29) | copy-start | bytes 98308
  238.9 47.4 %collective-permute-start.19 = (bf16[2048,768]{1,0:T(8,128)(2,1)}, bf16[2048,768]{1,0:T(8,128)(2,1)}, u32[]{:S(2)}, u32[]{:S(2)}) collective-permute-start(bf16[2048,768]{1,0:T(8,128)(2,1)} %get-tuple-element.150), channel_id=1, source_target_pairs={{0,1},{1,0},{2,3},{3,2},{4,5},{5,4},{6,7},{7,6},{8,9},{9,8},{10,11... | collective-permute-start | bytes 9437192 | tf_op jit(solution)/shard_map/ppermute | solution.py:1114
  286.2 261.4 %collective-permute-start.24 = (bf16[2048,768]{1,0:T(8,128)(2,1)}, bf16[2048,768]{1,0:T(8,128)(2,1)}, u32[]{:S(2)}, u32[]{:S(2)}) collective-permute-start(bf16[2048,768]{1,0:T(8,128)(2,1)} %get-tuple-element.170), channel_id=1, source_target_pairs={{0,1},{1,0},{2,3},{3,2},{4,5},{5,4},{6,7},{7,6},{8,9},{9,8},{10,11... | collective-permute-start | bytes 9437192 | tf_op jit(solution)/shard_map/ppermute | solution.py:1114
  506.7 54.2 %collective-permute-start.23 = (bf16[512,768]{1,0:T(8,128)(2,1)S(1)}, bf16[512,768]{1,0:T(8,128)(2,1)S(1)}, u32[]{:S(2)}, u32[]{:S(2)}) collective-permute-start(bf16[512,768]{1,0:T(8,128)(2,1)S(1)} %get-tuple-element.217), channel_id=1, source_target_pairs={{0,8},{2,10},{4,12},{6,14},{8,16},{10,18},{12,20},{14,22},{16,24},... | collective-permute-start | bytes 2359304 | tf_op jit(solution)/shard_map/ppermute | solution.py:1110
  510.2 56.5 %collective-permute-start.22 = (bf16[512,768]{1,0:T(8,128)(2,1)S(1)}, bf16[512,768]{1,0:T(8,128)(2,1)}, u32[]{:S(2)}, u32[]{:S(2)}) collective-permute-start(bf16[512,768]{1,0:T(8,128)(2,1)S(1)} %get-tuple-element.218), channel_id=1, source_target_pairs={{0,6},{2,8},{4,10},{6,12},{8,14},{10,16},{12,18},{14,20},{16,22},{... | collective-permute-start | bytes 2359304 | tf_op jit(solution)/shard_map/ppermute | solution.py:1110
  515.4 52.6 %collective-permute-start.21 = (bf16[512,768]{1,0:T(8,128)(2,1)S(1)}, bf16[512,768]{1,0:T(8,128)(2,1)}, u32[]{:S(2)}, u32[]{:S(2)}) collective-permute-start(bf16[512,768]{1,0:T(8,128)(2,1)S(1)} %get-tuple-element.219), channel_id=1, source_target_pairs={{6,0},{8,2},{10,4},{12,6},{14,8},{16,10},{18,12},{20,14},{22,16},{... | collective-permute-start | bytes 2359304 | tf_op jit(solution)/shard_map/ppermute | solution.py:1110
  516.7 52.6 %collective-permute-start.20 = (bf16[512,768]{1,0:T(8,128)(2,1)S(1)}, bf16[512,768]{1,0:T(8,128)(2,1)}, u32[]{:S(2)}, u32[]{:S(2)}) collective-permute-start(bf16[512,768]{1,0:T(8,128)(2,1)S(1)} %get-tuple-element.220), channel_id=1, source_target_pairs={{8,0},{10,2},{12,4},{14,6},{16,8},{18,10},{20,12},{22,14},{24,16},... | collective-permute-start | bytes 2359304 | tf_op jit(solution)/shard_map/ppermute | solution.py:1110
  518.0 26.0 %copy-start.4 = (bf16[1920,768]{1,0:T(8,128)(2,1)S(1)}, bf16[1920,768]{1,0:T(8,128)(2,1)}, u32[]{:S(2)}) copy-start(bf16[1920,768]{1,0:T(8,128)(2,1)} %get-tuple-element.193) | copy-start | bytes 8847364
  551.2 55.8 %collective-permute-start.29 = (bf16[512,768]{1,0:T(8,128)(2,1)S(1)}, bf16[512,768]{1,0:T(8,128)(2,1)}, u32[]{:S(2)}, u32[]{:S(2)}) collective-permute-start(bf16[512,768]{1,0:T(8,128)(2,1)S(1)} %get-tuple-element.213), channel_id=1, source_target_pairs={{0,4},{2,6},{4,8},{6,10},{8,12},{10,14},{12,16},{14,18},{16,20},{1... | collective-permute-start | bytes 2359304 | tf_op jit(solution)/shard_map/ppermute | solution.py:1110
  561.0 23.8 %copy-start.26 = (bf16[512,768]{1,0:T(8,128)(2,1)}, bf16[512,768]{1,0:T(8,128)(2,1)S(1)}, u32[]{:S(2)}) copy-start(bf16[512,768]{1,0:T(8,128)(2,1)S(1)} %collective-permute-done.23) | copy-start | bytes 2359300
  561.0 46.0 %collective-permute-start.28 = (bf16[512,768]{1,0:T(8,128)(2,1)S(1)}, bf16[512,768]{1,0:T(8,128)(2,1)}, u32[]{:S(2)}, u32[]{:S(2)}) collective-permute-start(bf16[512,768]{1,0:T(8,128)(2,1)S(1)} %get-tuple-element.214), channel_id=1, source_target_pairs={{0,2},{2,4},{4,6},{6,8},{8,10},{10,12},{12,14},{14,16},{16,18},{18... | collective-permute-start | bytes 2359304 | tf_op jit(solution)/shard_map/ppermute | solution.py:1110
  566.7 40.3 %collective-permute-start.27 = (bf16[512,768]{1,0:T(8,128)(2,1)S(1)}, bf16[512,768]{1,0:T(8,128)(2,1)}, u32[]{:S(2)}, u32[]{:S(2)}) collective-permute-start(bf16[512,768]{1,0:T(8,128)(2,1)S(1)} %get-tuple-element.215), channel_id=1, source_target_pairs={{2,0},{4,2},{6,4},{8,6},{10,8},{12,10},{14,12},{16,14},{18,16},{20... | collective-permute-start | bytes 2359304 | tf_op jit(solution)/shard_map/ppermute | solution.py:1110
  568.0 39.0 %collective-permute-start.26 = (bf16[512,768]{1,0:T(8,128)(2,1)S(1)}, bf16[512,768]{1,0:T(8,128)(2,1)}, u32[]{:S(2)}, u32[]{:S(2)}) collective-permute-start(bf16[512,768]{1,0:T(8,128)(2,1)S(1)} %get-tuple-element.216), channel_id=1, source_target_pairs={{4,0},{6,2},{8,4},{10,6},{12,8},{14,10},{16,12},{18,14},{20,16},{2... | collective-permute-start | bytes 2359304 | tf_op jit(solution)/shard_map/ppermute | solution.py:1110
  584.8 22.3 %copy-start.36 = (f32[768]{0:T(1024)S(1)}, f32[768]{0:T(1024)}, u32[]{:S(2)}) copy-start(f32[768]{0:T(1024)} %get-tuple-element.198) | copy-start | bytes 9220
  584.8 22.3 %copy-start.37 = (f32[768]{0:T(1024)S(1)}, f32[768]{0:T(1024)}, u32[]{:S(2)}) copy-start(f32[768]{0:T(1024)} %get-tuple-element.201) | copy-start | bytes 9220
  584.8 28.0 %collective-permute-start.25 = (bf16[512,768]{1,0:T(8,128)(2,1)}, bf16[512,768]{1,0:T(8,128)(2,1)}, u32[]{:S(2)}, u32[]{:S(2)}) collective-permute-start(bf16[512,768]{1,0:T(8,128)(2,1)} %get-tuple-element.175), channel_id=1, source_target_pairs={{0,1},{1,0},{2,3},{3,2},{4,5},{5,4},{6,7},{7,6},{8,9},{9,8},{10,11... | collective-permute-start | bytes 2359304 | tf_op jit(solution)/shard_map/ppermute | solution.py:1114
  617.9 66.9 %collective-permute-start.30 = (f32[512,768]{1,0:T(8,128)S(1)}, f32[512,768]{1,0:T(8,128)}, u32[]{:S(2)}, u32[]{:S(2)}) collective-permute-start(f32[512,768]{1,0:T(8,128)S(1)} %convert_add_fusion), channel_id=1, source_target_pairs={{0,1},{1,0},{2,3},{3,2},{4,5},{5,4},{6,7},{7,6},{8,9},{9,8},{10,11... | collective-permute-start | bytes 4718600 | tf_op jit(solution)/shard_map/ppermute | solution.py:1114
  (28 other events, 80.7 us)
Sparse Core Ops, SparseCore 0:
  213.7 289.4 all-reduce.7
where the time goes:
time: 712 us; the launch traced here: 699 us
  Pallas kernels  303 us (43%)
  waiting for transfers between devices  229 us (32%)
  starting transfers between devices  56.2 us (8%)
  other arithmetic  41.2 us (6%)
  local copies, waits for them, and re-layouts  35.3 us (5%)
  matrix products  17.8 us (2%)
  between operations  15.5 us (2%)
    psum x1, waiting for transfers between devices, body(): grad_up, down_out = lax.psum((grad_up_low, down_out_low), 'seq')  217 us
    pallas_call x1, Pallas kernels, sum_over_seq(): pl.pallas_call(partial(sum_kernel, n, streams, split), in_specs=[in_vmem,...  62.3 us
    pallas_call x3, Pallas kernels, attend(): pl.pallas_call(partial(attend_kernel, head_dim, tiles_k, seed is not None...  57.7 us
    ppermute x16, starting transfers between devices, shifted(): return lax.ppermute(block, axis, route)  52.4 us
    pallas_call x3, Pallas kernels, back_attend(): pl.pallas_call(partial(back_attend_kernel, head_dim, tiles_k, seed is not...  50.9 us
    pallas_call x3, Pallas kernels, back_project(): pl.pallas_call(partial(back_project_kernel, len(parts), turned, len(value...  41.4 us
    pallas_call x3, Pallas kernels, project(): pl.pallas_call(partial(project_kernel, units, count, head_dim), grid_spec...  24.2 us
    pallas_call x1, Pallas kernels, occupancy(): pl.pallas_call(partial(occupancy_kernel, hashes), grid=(pairs, tokens //...  19.6 us
  transfers between devices with their start and end apart: 32, of which 6 were waited for; matrix products, arithmetic and copies ran while one was open for 6% of the time, Pallas kernels for 38%

commit v1 on v0

--- a/solution.py
+++ b/solution.py
@@ -1255,15 +1255,9 @@
             chunk_tables[index], group_x[index], weight_kv, parts, 0, [dv], head_dim, **rims
         )
 
-    def send_home(distances, dx_mine, came):
-        both = [
-            (
-                dx_mine[i * half : (i + 1) * half].astype(F32)
-                + came[i * half : (i + 1) * half].astype(F32)
-            ).astype(BF16)
-            for i in range(len(distances))
-        ]
-        return both, [shifted(term, "seq", -d) for term, d in zip(both, distances)]
+    def both_sides(mine, came, first, number):
+        rows = slice(first * half, (first + number) * half)
+        return (mine[rows].astype(F32) + came[rows].astype(F32)).astype(BF16)
 
     dk, dv, turned = back_scores(far_at, grad_rows, None)
     far_dx, dx_other, far_dw = back_inputs(far_at, dk, dv)
@@ -1277,13 +1271,30 @@
         near_at, dk, dv, rims=close * (tokens // CHUNK) - 1, rim=rim
     )
     near_came = swapped(dx_other, "tp")
-    far_came, grad_up, down_out = after((far_came, grad_up, down_out), near_dx)
-    terms, far_homes = send_home(far, far_dx, far_came)
+    occ_local = occupancy(after(key_unit, near_dx), hyperplanes, 2.0**BITS / all_tokens)
+    far_came, near_came, grad_up, down_out = after(
+        (far_came, near_came, grad_up, down_out), occ_local
+    )
+    count = lax.axis_size("seq")
+    low_pair = both_sides(far_dx, far_came, 0, 2)
+    high_pair = both_sides(far_dx, far_came, 2, 2)
+    two_low, one_low, one_high, two_high = [
+        both_sides(near_dx, near_came, i, 1) for i in range(len(near))
+    ]
+    low_far = shifted(low_pair, "seq", -far_reach)
+    high_far = shifted(high_pair, "seq", far_reach)
+    last = count - far_reach
+    rest_home = lax.ppermute(
+        jnp.where(lax.axis_index("seq") == last, high_pair[:half], low_pair[half:]),
+        "seq",
+        [(far_reach - 1, 0), (last, count - 1)],
+    )
+    two_homes = [shifted(two_low, "seq", -close), shifted(two_high, "seq", close)]
     dk, dv, turned = back_attend(
         back_tables[own_at],
         k_counts[own_at],
         query_unit,
-        after(grad_rows, *terms),
+        after(grad_rows, low_pair, high_pair, two_low, one_low, one_high, two_high),
         key_unit,
         values,
         own_weights,
@@ -1291,8 +1302,13 @@
         seed=turned,
         cost=pl.CostEstimate(flops=1 << 35, bytes_accessed=1 << 20, transcendentals=0),
     )
-    terms, near_homes = send_home(near, near_dx, after(near_came, dk))
-    dk, key_late, far_homes = after((dk, key_unit, far_homes), *terms)
+    dk, low_far, high_far, rest_home, *two_homes = after(
+        (dk, low_far, high_far, rest_home, *two_homes), dv
+    )
+    one_low = (one_low.astype(F32) + high_far[:half].astype(F32)).astype(BF16)
+    one_high = (one_high.astype(F32) + low_far[half:].astype(F32)).astype(BF16)
+    one_homes = [shifted(one_low, "seq", -1), shifted(one_high, "seq", 1)]
+    dk = after(dk, one_low, one_high)
     own_mine = mine_rows
     own_other = lax.dynamic_slice_in_dim(inputs, (1 - my_side) * half, half, 0)
     dx_mine, dx_other, dw = back_project(
@@ -1305,8 +1321,8 @@
         head_dim,
     )
 
-    occ_local = occupancy(after(key_late, dw), hyperplanes, 2.0**BITS / all_tokens)
-    near_homes = after(tuple(near_homes), occ_local)
+    homes = [low_far[:half], high_far[half:], rest_home, *two_homes]
+    homes += after(tuple(one_homes), dw)
     qkv = jnp.concatenate([dw[:, :width], dw[:, width:] + near_dw + far_dw], axis=1).astype(BF16)
     misc = [
         occ_local,
@@ -1325,7 +1341,7 @@
         + dx_mine.astype(F32)
         + came.astype(F32)
     )
-    for home in (*far_homes, *near_homes):
+    for home in homes:
         total = total + home.astype(F32)
     other_total = swapped(total, "tp")
     lower = jnp.where(my_side == 0, total, other_total)

time: 712 us -> 702 us (0.986); the launches traced: 699 us -> 705 us
  waiting for transfers between devices: 229 us -> 237 us
    ppermute x16 -> x14, waiting for transfers between devices: 4.43 us -> 24.9 us  [shifted(): return lax.ppermute(block, axis, route)]
    psum x1, waiting for transfers between devices: 217 us -> 205 us  [body(): grad_up, down_out = lax.psum((grad_up_low, down_out_low), 'seq')]
    ppermute x16 -> x14, starting transfers between devices: 52.4 us -> 46.2 us  [shifted(): return lax.ppermute(block, axis, route)]
    unnamed x101 -> x107, local copies, waits for them, and re-layouts: 16.5 us -> 17.9 us
  transfers between devices with their start and end apart: 32 -> 31, of which waited for: 6 -> 10; matrix products, arithmetic and copies ran while one was open for 6% -> 5% of each run, Pallas kernels for 38% -> 38%
where the time goes in v1:
time: 702 us; the launch traced here: 705 us
  Pallas kernels  305 us (43%)
  waiting for transfers between devices  237 us (34%)
  starting transfers between devices  51.4 us (7%)
  other arithmetic  43.3 us (6%)
  local copies, waits for them, and re-layouts  34.5 us (5%)
  matrix products  17.9 us (3%)
  between operations  15.5 us (2%)
    psum x1, waiting for transfers between devices, body(): grad_up, down_out = lax.psum((grad_up_low, down_out_low), 'seq')  205 us
    pallas_call x1, Pallas kernels, sum_over_seq(): pl.pallas_call(partial(sum_kernel, n, streams, split), in_specs=[in_vmem,...  64.9 us
    pallas_call x3, Pallas kernels, attend(): pl.pallas_call(partial(attend_kernel, head_dim, tiles_k, seed is not None...  57.2 us
    pallas_call x3, Pallas kernels, back_attend(): pl.pallas_call(partial(back_attend_kernel, head_dim, tiles_k, seed is not...  51 us
    ppermute x14, starting transfers between devices, shifted(): return lax.ppermute(block, axis, route)  46.2 us
    pallas_call x3, Pallas kernels, back_project(): pl.pallas_call(partial(back_project_kernel, len(parts), turned, len(value...  41.4 us
    ppermute x14, waiting for transfers between devices, shifted(): return lax.ppermute(block, axis, route)  24.9 us
    pallas_call x3, Pallas kernels, project(): pl.pallas_call(partial(project_kernel, units, count, head_dim), grid_spec...  24.2 us
  transfers between devices with their start and end apart: 31, of which 10 were waited for; matrix products, arithmetic and copies ran while one was open for 5% of the time, Pallas kernels for 38%

profile of v1, /device:TPU:0, one launch (start us, length us, event | category | flops | bytes accessed | tf_op | source)
XLA Modules:
  0.0 705.3 jit_solution(11630149606914895531)
XLA Ops:
  7.3 2.5 constant_dynamic-slice_fusion
  12.3 5.5 collective-permute-start.2
  17.9 4.6 collective-permute-start.1
  22.5 12.3 %plan.1 = (s32[29]{0:T(128)}, s32[33]{0:T(128)}, s32[24]{0:T(128)}, s32[16]{0:T(128)}, s32[8]{0:T(128)}, /*index=5*/s32[29]{0:T(128)}, s32[33]{0:T(128)}, s32[24...) custom-call(s32[32]{0:T(128)} %length_ref.1), custom_call_target="tpu_custom_call" | custom-call | flops 1048576 | bytes 65536 | tf_op jit(solution)/shard_map/plan/pallas_call | solution.py:1093
  37.4 7.4 %project.3 = (bf16[1024,384]{1,0:T(8,128)(2,1)}, f32[1024,384]{1,0:T(8,128)}, bf16[1024,384]{1,0:T(8,128)(2,1)}, f32[1024,384]{1,0:T(8,128)}, bf16[1024,384]{1,0:T(8,128)(2,1)}) custom-call(s32[4]{0:T(128)} %constant.121.clone.table, bf16[1024,768]{1,0:T(8,128)(2,1)} %refs_0_.1, bf16[768,1152]{1,0:T(8,128)(2,1)} %copy-done.11), custom_call_target="tpu_custom_call" | custom-call | flops 3623878656 | bytes 786432 | tf_op jit(solution)/shard_map/project/pallas_call | solution.py:138
  44.8 31.0 %attend.3 = (f32[384,1024]{1,0:T(8,128)}, bf16[6,1024,1024]{2,1,0:T(8,128)(2,1)}) custom-call(s32[11]{0:T(128)} %get-tuple-element.109.table, bf16[1024,384]{1,0:T(8,128)(2,1)} %get-tuple-element.105.q_ref.refs_3_, s32[2,512]{1,0:T(2,128)} %get-tuple-element.106.qrow_ref, s32[2,512]{1,0:T(2,128)} %get-tuple-element.110.krow_ref, ...), custom_call_target="tpu_custom_call" | custom-call | flops 12884901888 | bytes 1572864 | tf_op jit(solution)/shard_map/attend/pallas_call | solution.py:252
  76.9 5.6 collective-permute-start
  85.3 7.1 %collective-permute-start.5 = (bf16[512,768]{1,0:T(8,128)(2,1)S(1)}, bf16[512,768]{1,0:T(8,128)(2,1)}, u32[]{:S(2)}, u32[]{:S(2)}) collective-permute-start(bf16[512,768]{1,0:T(8,128)(2,1)S(1)} %get-tuple-element.114.refs_0_), channel_id=1, source_target_pairs={{0,6},{2,8},{4,10},{6,12},{8,14},{10,16},{12,18},{14,20},{16,22},{... | collective-permute-start | bytes 2359304 | tf_op jit(solution)/shard_map/ppermute | solution.py:1110
  94.2 9.4 %project.4 = (bf16[4608,384]{1,0:T(8,128)(2,1)}, f32[4608,384]{1,0:T(8,128)}, bf16[4608,384]{1,0:T(8,128)(2,1)}) custom-call(s32[16]{0:T(128)} %get-tuple-element.117.table, bf16[512,768]{1,0:T(8,128)(2,1)} %copy-done.30, bf16[512,768]{1,0:T(8,128)(2,1)} %copy-done.29, bf16[512,768]{1,0:T(8,128)(2,1)} %copy-done.28, bf16[512,768]{1,0:T(8,128)(2,1)} %copy-done.27, ...), custom_call_target="tpu_custom_call" | custom-call | flops 9663676416 | bytes 3145728 | tf_op jit(solution)/shard_map/project/pallas_call | solution.py:138
  103.6 16.8 %attend.4 = (f32[384,1024]{1,0:T(8,128)}, bf16[6,4096,1024]{2,1,0:T(8,128)(2,1)}) custom-call(s32[29]{0:T(128)} %get-tuple-element.115.table, bf16[1024,384]{1,0:T(8,128)(2,1)} %get-tuple-element.105.q_ref.refs_3_, s32[2,512]{1,0:T(2,128)} %get-tuple-element.106.qrow_ref, s32[8,512]{1,0:T(8,128)} %get-tuple-element.116.krow_ref, ...), custom_call_target="tpu_custom_call" | custom-call | flops 51539607552 | bytes 1572864 | tf_op jit(solution)/shard_map/attend/pallas_call | solution.py:252
  120.4 4.5 collective-permute-done.5.refs_1_
  132.4 7.4 %project.5 = (bf16[4608,384]{1,0:T(8,128)(2,1)}, f32[4608,384]{1,0:T(8,128)}, bf16[4608,384]{1,0:T(8,128)(2,1)}) custom-call(s32[16]{0:T(128)} %get-tuple-element.108.table, bf16[512,768]{1,0:T(8,128)(2,1)} %collective-permute-done.refs_0_, bf16[512,768]{1,0:T(8,128)(2,1)} %collective-permute-done.5.refs_1_, ...), custom_call_target="tpu_custom_call" | custom-call | flops 9663676416 | bytes 3145728 | tf_op jit(solution)/shard_map/project/pallas_call | solution.py:138
  139.8 9.5 %attend.5 = (f32[384,1024]{1,0:T(8,128)}, bf16[6,4096,1024]{2,1,0:T(8,128)(2,1)}) custom-call(s32[29]{0:T(128)} %get-tuple-element.104.table, bf16[1024,384]{1,0:T(8,128)(2,1)} %get-tuple-element.105.q_ref.refs_3_, s32[2,512]{1,0:T(2,128)} %get-tuple-element.106.qrow_ref, s32[8,512]{1,0:T(8,128)} %get-tuple-element.107.krow_ref, ...), custom_call_target="tpu_custom_call" | custom-call | flops 51539607552 | bytes 1572864 | tf_op jit(solution)/shard_map/attend/pallas_call | solution.py:252
  149.3 8.2 %mix.1 = bf16[1024,384]{1,0:T(8,128)(2,1)} custom-call(f32[384,1024]{1,0:T(8,128)} %get-tuple-element.131.g_ref, s32[1536,128]{1,0:T(8,128)} %get-tuple-element.132.col_ref, bf16[1024,384]{1,0:T(8,128)(2,1)} %get-tuple-element.112.v_ref, bf16[32,384]{1,0:T(8,128)(2,1)} %slice_select_fusion.1.rim_ref, s32[8,256]{1,0:T(8,128)} %get-tuple-element.134.row_ref, ...), custom_call_target="tpu_custom_call" | custom-call | flops 1048576 | bytes 65536 | tf_op jit(solution)/shard_map/mix/pallas_call | solution.py:537
  157.5 2.1 convolution_convert_fusion.2
  159.8 3.3 collective-permute-done.16
  166.2 12.8 %feed.1 = (bf16[1024,768]{1,0:T(8,128)(2,1)}, bf16[1024,1536]{1,0:T(8,128)(2,1)}, bf16[1024,1536]{1,0:T(8,128)(2,1)}) custom-call(bf16[1024,768]{1,0:T(8,128)(2,1)} %fusion.4.x_ref, bf16[768,1536]{1,0:T(8,128)(2,1)} %up_ref.1, bf16[1536,768]{1,0:T(8,128)(2,1)} %down_ref.1), custom_call_target="tpu_custom_call" | custom-call | flops 1048576 | bytes 65536 | tf_op jit(solution)/shard_map/feed/pallas_call | solution.py:778
  179.2 3.5 collective-permute-done.17
  182.6 2.6 fusion.18
  188.0 2.6 fusion.17
  191.1 3.0 multiply_convert_fusion
  194.1 2.6 convolution_convert_fusion.3
  197.0 4.2 convolution_convert_fusion.1
  201.2 3.3 convolution_convert_fusion
  204.5 2.1 multiply_reduce_fusion
  210.9 1.9 convolution_convert_fusion.4.m_ref
  216.5 3.6 back_norm.1.g_ref
  220.1 10.6 %back_attend.3 = (bf16[4096,384]{1,0:T(8,128)(2,1)}, bf16[4096,384]{1,0:T(8,128)(2,1)}, f32[384,1024]{1,0:T(8,128)}) custom-call(s32[33]{0:T(128)} %get-tuple-element.144.table, bf16[1024,384]{1,0:T(8,128)(2,1)} %get-tuple-element.105.q_ref.refs_3_, bf16[1024,384]{1,0:T(8,128)(2,1)} %back_norm.1.g_ref, bf16[4608,384]{1,0:T(8,128)(2,1)} %get-tuple-element.129.k_ref.refs_6_, ...), custom_call_target="tpu_custom_call" | custom-call | flops 1048576 | bytes 65536 | tf_op jit(solution)/shard_map/back_attend/pallas_call | solution.py:349
  230.7 11.0 %back_project.3 = (bf16[2048,768]{1,0:T(8,128)(2,1)}, bf16[2048,768]{1,0:T(8,128)(2,1)}, f32[768,768]{1,0:T(8,128)}) custom-call(s32[24]{0:T(128)} %get-tuple-element.142.table, bf16[512,768]{1,0:T(8,128)(2,1)} %collective-permute-done.refs_0_, bf16[512,768]{1,0:T(8,128)(2,1)} %collective-permute-done.5.refs_1_, ...), custom_call_target="tpu_custom_call" | custom-call | flops 1048576 | bytes 65536 | tf_op jit(solution)/shard_map/back_project/pallas_call | solution.py:455
  241.7 10.2 %back_conv.1 = (f32[1280,384]{1,0:T(8,128)}, f32[8,256]{1,0:T(8,128)}) custom-call(s32[1536,128]{1,0:T(8,128)} %get-tuple-element.132.col_ref, bf16[1024,384]{1,0:T(8,128)(2,1)} %get-tuple-element.112.v_ref, bf16[32,384]{1,0:T(8,128)(2,1)} %slice_select_fusion.1.rim_ref, bf16[1024,384]{1,0:T(8,128)(2,1)} %convolution_convert_fusion.4.m_ref, ...), custom_call_target="tpu_custom_call" | custom-call | flops 1048576 | bytes 65536 | tf_op jit(solution)/shard_map/back_conv/pallas_call | solution.py:632
  251.9 14.4 %back_attend.4 = (bf16[4096,384]{1,0:T(8,128)(2,1)}, bf16[4096,384]{1,0:T(8,128)(2,1)}, f32[384,1024]{1,0:T(8,128)}) custom-call(s32[33]{0:T(128)} %get-tuple-element.152.table, bf16[1024,384]{1,0:T(8,128)(2,1)} %get-tuple-element.105.q_ref.refs_3_, bf16[1024,384]{1,0:T(8,128)(2,1)} %back_norm.1.g_ref, bf16[4608,384]{1,0:T(8,128)(2,1)} %get-tuple-element.122.k_ref.refs_6_, ...), custom_call_target="tpu_custom_call" | custom-call | flops 1048576 | bytes 65536 | tf_op jit(solution)/shard_map/back_attend/pallas_call | solution.py:349
  267.1 14.9 %back_project.4 = (bf16[2048,768]{1,0:T(8,128)(2,1)}, bf16[2048,768]{1,0:T(8,128)(2,1)}, f32[768,768]{1,0:T(8,128)}) custom-call(s32[24]{0:T(128)} %get-tuple-element.150.table, bf16[512,768]{1,0:T(8,128)(2,1)} %copy-done.30, bf16[512,768]{1,0:T(8,128)(2,1)} %copy-done.29, bf16[512,768]{1,0:T(8,128)(2,1)} %copy-done.28, bf16[512,768]{1,0:T(8,128)(2,1)} %copy-done.27, ...), custom_call_target="tpu_custom_call" | custom-call | flops 1048576 | bytes 65536 | tf_op jit(solution)/shard_map/back_project/pallas_call | solution.py:455
  284.8 19.6 %occupancy.1 = f32[6,32,256]{2,1,0:T(8,128)} custom-call(bf16[1024,384]{1,0:T(8,128)(2,1)} %get-tuple-element.163.k_ref.refs_6_, bf16[2,128,1024]{2,1,0:T(8,128)(2,1)} %pad_maximum_fusion.3.w_ref), custom_call_target="tpu_custom_call" | custom-call | flops 12582912000 | bytes 1572864 | tf_op jit(solution)/shard_map/occupancy/pallas_call | solution.py:733
  305.3 204.5 %all-reduce.8.cloned.1.call-done = (bf16[768,1536]{1,0:T(8,128)(2,1)}, bf16[1920,768]{1,0:T(8,128)(2,1)}) async-done(((bf16[768,1536]{1,0:T(8,128)(2,1)}, bf16[1920,768]{1,0:T(8,128)(2,1)}), (bf16[768,1536]{1,0:T(8,128)(2,1)}, bf16[1920,768]{1,0:T(8,128)(2,1)})) %all-reduce.8.cloned.1.call-update) | async-done | bytes 5308432 | tf_op jit(solution)/shard_map/psum | solution.py:1233
  509.9 3.7 add_convert_fusion
  513.6 3.8 add_convert_fusion.7
  517.4 3.4 collective-permute-start.25
  522.1 5.5 collective-permute-start.22
  531.2 26.0 %back_attend.5 = (bf16[1024,384]{1,0:T(8,128)(2,1)}, bf16[1024,384]{1,0:T(8,128)(2,1)}, f32[384,1024]{1,0:T(8,128)}) custom-call(s32[15]{0:T(128)} %get-tuple-element.139.table, bf16[1024,384]{1,0:T(8,128)(2,1)} %get-tuple-element.105.q_ref.refs_3_, bf16[1024,384]{1,0:T(8,128)(2,1)} %back_norm.1.g_ref, bf16[1024,384]{1,0:T(8,128)(2,1)} %get-tuple-element.163.k_ref.refs_6_, ...), custom_call_target="tpu_custom_call" | custom-call | flops 34359738368 | bytes 1048576 | tf_op jit(solution)/shard_map/back_attend/pallas_call | solution.py:349
  560.4 16.0 %collective-permute-done.21 = bf16[1024,768]{1,0:T(8,128)(2,1)} collective-permute-done((bf16[1024,768]{1,0:T(8,128)(2,1)S(1)}, bf16[1024,768]{1,0:T(8,128)(2,1)}, u32[]{:S(2)}, u32[]{:S(2)}) %collective-permute-start.21) | collective-permute-done | bytes 1572896 | tf_op jit(solution)/shard_map/ppermute | solution.py:1110
  576.5 2.2 add_convert_fusion.5
  581.0 5.5 collective-permute-start.28
  586.6 15.5 %back_project.5 = (bf16[512,768]{1,0:T(8,128)(2,1)}, bf16[512,768]{1,0:T(8,128)(2,1)}, f32[768,1152]{1,0:T(8,128)}) custom-call(s32[6]{0:T(128)} %get-tuple-element.137.table, bf16[512,768]{1,0:T(8,128)(2,1)} %copy-done.12, bf16[512,768]{1,0:T(8,128)(2,1)} %get-tuple-element.222.refs_1_, bf16[768,1152]{1,0:T(8,128)(2,1)} %copy-done.11, ...), custom_call_target="tpu_custom_call" | custom-call | flops 1048576 | bytes 65536 | tf_op jit(solution)/shard_map/back_project/pallas_call | solution.py:455
  603.1 2.3 concatenate.49
  607.2 2.5 slice.195
  609.7 3.0 convert_element_type.266
  618.5 3.4 convert_add_fusion
  622.4 64.9 %sum_over_seq.1 = (f32[768,384]{1,0:T(8,128)}, f32[768,384]{1,0:T(8,128)}, f32[768,384]{1,0:T(8,128)}, f32[128,512]{1,0:T(8,128)}) custom-call(bf16[768,1152]{1,0:T(8,128)(2,1)} %pad_maximum_fusion.2.refs_0_, f32[128,512]{1,0:T(8,128)} %reshape.195.refs_1_), custom_call_target="tpu_custom_call" | custom-call | flops 68719476736 | bytes 16777216 | tf_op jit(solution)/shard_map/sum_over_seq/pallas_call | solution.py:950
  (239 shorter events, 67.6 us)
Async XLA Ops:
  7.2 150.3 %copy-start = (bf16[384,768]{1,0:T(8,128)(2,1)S(1)}, bf16[384,768]{1,0:T(8,128)(2,1)}, u32[]{:S(2)}) copy-start(bf16[384,768]{1,0:T(8,128)(2,1)} %param.21) | copy-start | bytes 1769476
  7.2 27.6 %copy-start.36 = (bf16[768,384]{1,0:T(8,128)(2,1)S(1)}, bf16[768,384]{1,0:T(8,128)(2,1)}, u32[]{:S(2)}) copy-start(bf16[768,384]{1,0:T(8,128)(2,1)} %param.18) | copy-start | bytes 1769476
  7.2 27.7 %copy-start.34 = (bf16[768,384]{1,0:T(8,128)(2,1)S(1)}, bf16[768,384]{1,0:T(8,128)(2,1)}, u32[]{:S(2)}) copy-start(bf16[768,384]{1,0:T(8,128)(2,1)} %param.19) | copy-start | bytes 1769476
  7.2 502.6 %all-reduce.8.cloned.1.call-start = ((), (), s32[]{:S(2)}) async-start(), calls=%async_computation | async-start | bytes 10616832 | tf_op jit(solution)/shard_map/psum | solution.py:1233
  9.8 75.5 %copy-start.12 = (bf16[512,768]{1,0:T(8,128)(2,1)}, bf16[512,768]{1,0:T(8,128)(2,1)S(1)}, u32[]{:S(2)}) copy-start(bf16[512,768]{1,0:T(8,128)(2,1)S(1)} %get-tuple-element.114.refs_0_) | copy-start | bytes 2359300
  9.8 66.0 %collective-permute-start.4 = (bf16[512,768]{1,0:T(8,128)(2,1)S(1)}, bf16[512,768]{1,0:T(8,128)(2,1)S(1)}, u32[]{:S(2)}, u32[]{:S(2)}) collective-permute-start(bf16[512,768]{1,0:T(8,128)(2,1)S(1)} %get-tuple-element.114.refs_0_), channel_id=1, source_target_pairs={{4,0},{6,2},{8,4},{10,6},{12,8},{14,10},{16,12},{18,14},{20,16},{2... | collective-permute-start | bytes 2359304 | tf_op jit(solution)/shard_map/ppermute | solution.py:1110
  11.0 64.7 %collective-permute-start.3 = (bf16[512,768]{1,0:T(8,128)(2,1)S(1)}, bf16[512,768]{1,0:T(8,128)(2,1)S(1)}, u32[]{:S(2)}, u32[]{:S(2)}) collective-permute-start(bf16[512,768]{1,0:T(8,128)(2,1)S(1)} %get-tuple-element.114.refs_0_), channel_id=1, source_target_pairs={{2,0},{4,2},{6,4},{8,6},{10,8},{12,10},{14,12},{16,14},{18,16},{20... | collective-permute-start | bytes 2359304 | tf_op jit(solution)/shard_map/ppermute | solution.py:1110
  12.3 63.4 %collective-permute-start.2 = (bf16[512,768]{1,0:T(8,128)(2,1)S(1)}, bf16[512,768]{1,0:T(8,128)(2,1)S(1)}, u32[]{:S(2)}, u32[]{:S(2)}) collective-permute-start(bf16[512,768]{1,0:T(8,128)(2,1)S(1)} %get-tuple-element.114.refs_0_), channel_id=1, source_target_pairs={{0,2},{2,4},{4,6},{6,8},{8,10},{10,12},{12,14},{14,16},{16,18},{18... | collective-permute-start | bytes 2359304 | tf_op jit(solution)/shard_map/ppermute | solution.py:1110
  17.9 57.9 %collective-permute-start.1 = (bf16[512,768]{1,0:T(8,128)(2,1)S(1)}, bf16[512,768]{1,0:T(8,128)(2,1)S(1)}, u32[]{:S(2)}, u32[]{:S(2)}) collective-permute-start(bf16[512,768]{1,0:T(8,128)(2,1)S(1)} %get-tuple-element.114.refs_0_), channel_id=1, source_target_pairs={{0,4},{2,6},{4,8},{6,10},{8,12},{10,14},{12,16},{14,18},{16,20},{1... | collective-permute-start | bytes 2359304 | tf_op jit(solution)/shard_map/ppermute | solution.py:1110
  36.1 8.7 %copy-start.5 = (bf16[768,768]{1,0:T(8,128)(2,1)}, bf16[768,768]{1,0:T(8,128)(2,1)S(1)}, u32[]{:S(2)}) copy-start(bf16[768,768]{1,0:T(8,128)(2,1)S(1)} %get-tuple-element.224.refs_5_) | copy-start | bytes 3538948
  75.8 16.7 %copy-start.27 = (bf16[512,768]{1,0:T(8,128)(2,1)}, bf16[512,768]{1,0:T(8,128)(2,1)S(1)}, u32[]{:S(2)}) copy-start(bf16[512,768]{1,0:T(8,128)(2,1)S(1)} %collective-permute-done.4.refs_3_) | copy-start | bytes 2359300
  75.8 16.7 %copy-start.28 = (bf16[512,768]{1,0:T(8,128)(2,1)}, bf16[512,768]{1,0:T(8,128)(2,1)S(1)}, u32[]{:S(2)}) copy-start(bf16[512,768]{1,0:T(8,128)(2,1)S(1)} %collective-permute-done.3.refs_2_) | copy-start | bytes 2359300
  75.8 16.7 %copy-start.29 = (bf16[512,768]{1,0:T(8,128)(2,1)}, bf16[512,768]{1,0:T(8,128)(2,1)S(1)}, u32[]{:S(2)}) copy-start(bf16[512,768]{1,0:T(8,128)(2,1)S(1)} %collective-permute-done.2.refs_1_) | copy-start | bytes 2359300
  75.8 16.7 %copy-start.30 = (bf16[512,768]{1,0:T(8,128)(2,1)}, bf16[512,768]{1,0:T(8,128)(2,1)S(1)}, u32[]{:S(2)}) copy-start(bf16[512,768]{1,0:T(8,128)(2,1)S(1)} %collective-permute-done.1.refs_0_) | copy-start | bytes 2359300
  75.8 6.7 collective-permute-start.8
  75.9 8.0 %collective-permute-start.9 = (bf16[512,768]{1,0:T(8,128)(2,1)S(1)}, bf16[512,768]{1,0:T(8,128)(2,1)S(1)}, u32[]{:S(2)}, u32[]{:S(2)}) collective-permute-start(bf16[512,768]{1,0:T(8,128)(2,1)S(1)} %collective-permute-done.2.refs_1_), channel_id=1, source_target_pairs={{0,1},{1,0},{2,3},{3,2},{4,5},{5,4},{6,7},{7,6},{8,9},{9,8},{10,11... | collective-permute-start | bytes 2359304 | tf_op jit(solution)/shard_map/ppermute | solution.py:1114
  76.4 8.9 %collective-permute-start.10 = (bf16[512,768]{1,0:T(8,128)(2,1)S(1)}, bf16[512,768]{1,0:T(8,128)(2,1)S(1)}, u32[]{:S(2)}, u32[]{:S(2)}) collective-permute-start(bf16[512,768]{1,0:T(8,128)(2,1)S(1)} %collective-permute-done.3.refs_2_), channel_id=1, source_target_pairs={{0,1},{1,0},{2,3},{3,2},{4,5},{5,4},{6,7},{7,6},{8,9},{9,8},{10,11... | collective-permute-start | bytes 2359304 | tf_op jit(solution)/shard_map/ppermute | solution.py:1114
  76.5 15.9 %collective-permute-start.11 = (bf16[512,768]{1,0:T(8,128)(2,1)S(1)}, bf16[512,768]{1,0:T(8,128)(2,1)S(1)}, u32[]{:S(2)}, u32[]{:S(2)}) collective-permute-start(bf16[512,768]{1,0:T(8,128)(2,1)S(1)} %collective-permute-done.4.refs_3_), channel_id=1, source_target_pairs={{0,1},{1,0},{2,3},{3,2},{4,5},{5,4},{6,7},{7,6},{8,9},{9,8},{10,11... | collective-permute-start | bytes 2359304 | tf_op jit(solution)/shard_map/ppermute | solution.py:1114
  76.9 43.5 %collective-permute-start = (bf16[512,768]{1,0:T(8,128)(2,1)S(1)}, bf16[512,768]{1,0:T(8,128)(2,1)}, u32[]{:S(2)}, u32[]{:S(2)}) collective-permute-start(bf16[512,768]{1,0:T(8,128)(2,1)S(1)} %get-tuple-element.114.refs_0_), channel_id=1, source_target_pairs={{0,8},{2,10},{4,12},{6,14},{8,16},{10,18},{12,20},{14,22},{16,24},... | collective-permute-start | bytes 2359304 | tf_op jit(solution)/shard_map/ppermute | solution.py:1110
  82.5 37.9 %collective-permute-start.7 = (bf16[512,768]{1,0:T(8,128)(2,1)S(1)}, bf16[512,768]{1,0:T(8,128)(2,1)}, u32[]{:S(2)}, u32[]{:S(2)}) collective-permute-start(bf16[512,768]{1,0:T(8,128)(2,1)S(1)} %get-tuple-element.114.refs_0_), channel_id=1, source_target_pairs={{8,0},{10,2},{12,4},{14,6},{16,8},{18,10},{20,12},{22,14},{24,16},... | collective-permute-start | bytes 2359304 | tf_op jit(solution)/shard_map/ppermute | solution.py:1110
  83.9 36.5 %collective-permute-start.6 = (bf16[512,768]{1,0:T(8,128)(2,1)S(1)}, bf16[512,768]{1,0:T(8,128)(2,1)}, u32[]{:S(2)}, u32[]{:S(2)}) collective-permute-start(bf16[512,768]{1,0:T(8,128)(2,1)S(1)} %get-tuple-element.114.refs_0_), channel_id=1, source_target_pairs={{6,0},{8,2},{10,4},{12,6},{14,8},{16,10},{18,12},{20,14},{22,16},{... | collective-permute-start | bytes 2359304 | tf_op jit(solution)/shard_map/ppermute | solution.py:1110
  85.3 39.6 %collective-permute-start.5 = (bf16[512,768]{1,0:T(8,128)(2,1)S(1)}, bf16[512,768]{1,0:T(8,128)(2,1)}, u32[]{:S(2)}, u32[]{:S(2)}) collective-permute-start(bf16[512,768]{1,0:T(8,128)(2,1)S(1)} %get-tuple-element.114.refs_0_), channel_id=1, source_target_pairs={{0,6},{2,8},{4,10},{6,12},{8,14},{10,16},{12,18},{14,20},{16,22},{... | collective-permute-start | bytes 2359304 | tf_op jit(solution)/shard_map/ppermute | solution.py:1110
  103.6 22.3 %copy-start.46 = (s32[8]{0:T(128)S(1)}, s32[8]{0:T(128)}, u32[]{:S(2)}) copy-start(s32[8]{0:T(128)} %get-tuple-element.133) | copy-start | bytes 100
  103.6 22.5 %copy-start.41 = (f32[6,33]{1,0:T(8,128)S(1)}, f32[6,33]{1,0:T(8,128)}, u32[]{:S(2)}) copy-start(f32[6,33]{1,0:T(8,128)} %param.24) | copy-start | bytes 2380
  124.9 3.7 collective-permute-start.12
  124.9 4.9 collective-permute-start.13
  125.4 4.5 collective-permute-start.14
  125.4 5.4 collective-permute-start.15
  149.3 13.8 %copy-start.6 = (bf16[1024,768]{1,0:T(8,128)(2,1)S(1)}, bf16[1024,768]{1,0:T(8,128)(2,1)}, u32[]{:S(2)}) copy-start(bf16[1024,768]{1,0:T(8,128)(2,1)} %refs_0_.1) | copy-start | bytes 4718596
  159.6 3.5 collective-permute-start.16
  179.0 3.6 collective-permute-start.17
  196.8 7.7 %collective-permute-start.18 = (bf16[1024,768]{1,0:T(8,128)(2,1)S(1)}, bf16[1024,768]{1,0:T(8,128)(2,1)S(1)}, u32[]{:S(2)}, u32[]{:S(2)}) collective-permute-start(bf16[1024,768]{1,0:T(8,128)(2,1)S(1)} %convolution_convert_fusion.3), channel_id=1, source_target_pairs={{0,1},{1,0},{2,3},{3,2},{4,5},{5,4},{6,7},{7,6},{8,9},{9,8},{10,11... | collective-permute-start | bytes 4718600 | tf_op jit(solution)/shard_map/ppermute | solution.py:1114
  251.9 14.4 %copy-start.21 = (f32[1280,384]{1,0:T(8,128)S(1)}, f32[1280,384]{1,0:T(8,128)}, u32[]{:S(2)}) copy-start(f32[1280,384]{1,0:T(8,128)} %get-tuple-element.155) | copy-start | bytes 5898244
  281.9 23.4 %collective-permute-start.20 = (bf16[2048,768]{1,0:T(8,128)(2,1)}, bf16[2048,768]{1,0:T(8,128)(2,1)}, u32[]{:S(2)}, u32[]{:S(2)}) collective-permute-start(bf16[2048,768]{1,0:T(8,128)(2,1)} %get-tuple-element.161), channel_id=1, source_target_pairs={{0,1},{1,0},{2,3},{3,2},{4,5},{5,4},{6,7},{7,6},{8,9},{9,8},{10,11... | collective-permute-start | bytes 9437192 | tf_op jit(solution)/shard_map/ppermute | solution.py:1114
  282.0 23.3 %collective-permute-start.19 = (bf16[2048,768]{1,0:T(8,128)(2,1)}, bf16[2048,768]{1,0:T(8,128)(2,1)}, u32[]{:S(2)}, u32[]{:S(2)}) collective-permute-start(bf16[2048,768]{1,0:T(8,128)(2,1)} %get-tuple-element.149), channel_id=1, source_target_pairs={{0,1},{1,0},{2,3},{3,2},{4,5},{5,4},{6,7},{7,6},{8,9},{9,8},{10,11... | collective-permute-start | bytes 9437192 | tf_op jit(solution)/shard_map/ppermute | solution.py:1114
  517.4 39.8 %collective-permute-start.25 = (bf16[512,768]{1,0:T(8,128)(2,1)}, bf16[512,768]{1,0:T(8,128)(2,1)S(1)}, u32[]{:S(2)}, u32[]{:S(2)}) collective-permute-start(bf16[512,768]{1,0:T(8,128)(2,1)} %get-tuple-element.211), channel_id=1, source_target_pairs={{0,4},{2,6},{4,8},{6,10},{8,12},{10,14},{12,16},{14,18},{16,20},{1... | collective-permute-start | bytes 2359304 | tf_op jit(solution)/shard_map/ppermute | solution.py:1110
  520.8 37.9 %collective-permute-start.24 = (bf16[512,768]{1,0:T(8,128)(2,1)}, bf16[512,768]{1,0:T(8,128)(2,1)}, u32[]{:S(2)}, u32[]{:S(2)}) collective-permute-start(bf16[512,768]{1,0:T(8,128)(2,1)} %get-tuple-element.214), channel_id=1, source_target_pairs={{4,0},{6,2},{8,4},{10,6},{12,8},{14,10},{16,12},{18,14},{20,16},{2... | collective-permute-start | bytes 2359304 | tf_op jit(solution)/shard_map/ppermute | solution.py:1110
  522.1 38.3 %collective-permute-start.22 = (bf16[1024,768]{1,0:T(8,128)(2,1)S(1)}, bf16[1024,768]{1,0:T(8,128)(2,1)S(1)}, u32[]{:S(2)}, u32[]{:S(2)}) collective-permute-start(bf16[1024,768]{1,0:T(8,128)(2,1)S(1)} %get-tuple-element.215), channel_id=1, source_target_pairs={{0,8},{2,10},{4,12},{6,14},{8,16},{10,18},{12,20},{14,22},{16,24},... | collective-permute-start | bytes 4718600 | tf_op jit(solution)/shard_map/ppermute | solution.py:1110
  527.6 48.8 %collective-permute-start.21 = (bf16[1024,768]{1,0:T(8,128)(2,1)S(1)}, bf16[1024,768]{1,0:T(8,128)(2,1)}, u32[]{:S(2)}, u32[]{:S(2)}) collective-permute-start(bf16[1024,768]{1,0:T(8,128)(2,1)S(1)} %get-tuple-element.216), channel_id=1, source_target_pairs={{8,0},{10,2},{12,4},{14,6},{16,8},{18,10},{20,12},{22,14},{24,16},... | collective-permute-start | bytes 4718600 | tf_op jit(solution)/shard_map/ppermute | solution.py:1110
  529.9 27.3 %collective-permute-start.23 = (bf16[512,768]{1,0:T(8,128)(2,1)}, bf16[512,768]{1,0:T(8,128)(2,1)}, u32[]{:S(2)}, u32[]{:S(2)}) collective-permute-start(bf16[512,768]{1,0:T(8,128)(2,1)} %slice_select_fusion), channel_id=1, source_target_pairs={{6,0},{24,30},{7,1},{25,31}} | collective-permute-start | bytes 2359304 | tf_op jit(solution)/shard_map/ppermute | solution.py:1287
  557.2 29.3 %copy-start.31 = (bf16[512,768]{1,0:T(8,128)(2,1)}, bf16[512,768]{1,0:T(8,128)(2,1)S(1)}, u32[]{:S(2)}) copy-start(bf16[512,768]{1,0:T(8,128)(2,1)S(1)} %collective-permute-done.25) | copy-start | bytes 2359300
  560.4 26.1 %copy-start.22 = (bf16[1024,768]{1,0:T(8,128)(2,1)}, bf16[1024,768]{1,0:T(8,128)(2,1)S(1)}, u32[]{:S(2)}) copy-start(bf16[1024,768]{1,0:T(8,128)(2,1)S(1)} %collective-permute-done.22) | copy-start | bytes 4718596
  579.7 36.9 %collective-permute-start.27 = (bf16[512,768]{1,0:T(8,128)(2,1)}, bf16[512,768]{1,0:T(8,128)(2,1)}, u32[]{:S(2)}, u32[]{:S(2)}) collective-permute-start(bf16[512,768]{1,0:T(8,128)(2,1)} %add_convert_fusion.6), channel_id=1, source_target_pairs={{2,0},{4,2},{6,4},{8,6},{10,8},{12,10},{14,12},{16,14},{18,16},{20... | collective-permute-start | bytes 2359304 | tf_op jit(solution)/shard_map/ppermute | solution.py:1110
  581.0 36.9 %collective-permute-start.28 = (bf16[512,768]{1,0:T(8,128)(2,1)}, bf16[512,768]{1,0:T(8,128)(2,1)}, u32[]{:S(2)}, u32[]{:S(2)}) collective-permute-start(bf16[512,768]{1,0:T(8,128)(2,1)} %add_convert_fusion.5), channel_id=1, source_target_pairs={{0,2},{2,4},{4,6},{6,8},{8,10},{10,12},{12,14},{14,16},{16,18},{18... | collective-permute-start | bytes 2359304 | tf_op jit(solution)/shard_map/ppermute | solution.py:1110
  586.5 15.6 %copy-start.43 = (f32[8,256]{1,0:T(8,128)S(1)}, f32[8,256]{1,0:T(8,128)}, u32[]{:S(2)}) copy-start(f32[8,256]{1,0:T(8,128)} %get-tuple-element.187) | copy-start | bytes 24580
  586.5 19.5 %copy-start.4 = (bf16[1920,768]{1,0:T(8,128)(2,1)S(1)}, bf16[1920,768]{1,0:T(8,128)(2,1)}, u32[]{:S(2)}) copy-start(bf16[1920,768]{1,0:T(8,128)(2,1)} %get-tuple-element.191) | copy-start | bytes 8847364
  602.0 15.9 %collective-permute-start.26 = (bf16[512,768]{1,0:T(8,128)(2,1)}, bf16[512,768]{1,0:T(8,128)(2,1)}, u32[]{:S(2)}, u32[]{:S(2)}) collective-permute-start(bf16[512,768]{1,0:T(8,128)(2,1)} %get-tuple-element.178), channel_id=1, source_target_pairs={{0,1},{1,0},{2,3},{3,2},{4,5},{5,4},{6,7},{7,6},{8,9},{9,8},{10,11... | collective-permute-start | bytes 2359304 | tf_op jit(solution)/shard_map/ppermute | solution.py:1114
  621.9 69.5 %collective-permute-start.29 = (f32[512,768]{1,0:T(8,128)S(1)}, f32[512,768]{1,0:T(8,128)}, u32[]{:S(2)}, u32[]{:S(2)}) collective-permute-start(f32[512,768]{1,0:T(8,128)S(1)} %convert_add_fusion), channel_id=1, source_target_pairs={{0,1},{1,0},{2,3},{3,2},{4,5},{5,4},{6,7},{7,6},{8,9},{9,8},{10,11... | collective-permute-start | bytes 4718600 | tf_op jit(solution)/shard_map/ppermute | solution.py:1114
  (30 other events, 73.0 us)
Sparse Core Ops, SparseCore 0:
  214.7 295.1 all-reduce.7

commit v2 on v1

--- a/solution.py
+++ b/solution.py
@@ -1037,37 +1037,46 @@
         for i in range(number):
             need_ref[i] = need[i]
 
-    def ids_of(positions):
-        def step(doc, total):
-            return total + (end_ref[doc] <= positions).astype(jnp.int32)
-
-        total = lax.fori_loop(0, docs, step, jnp.zeros_like(positions))
-        total = jnp.where(positions < 0, -1, total)
-        return jnp.where(positions >= all_tokens, FAR_ID, total)
+    def ids_of(arrays):
+        def step(doc, totals):
+            end = end_ref[doc]
+            return [
+                total + (end <= positions).astype(jnp.int32)
+                for total, positions in zip(totals, arrays)
+            ]
+
+        totals = lax.fori_loop(0, docs, step, [jnp.zeros_like(a) for a in arrays])
+        return [
+            jnp.where(
+                positions < 0, -1, jnp.where(positions >= all_tokens, FAR_ID, total)
+            )
+            for total, positions in zip(totals, arrays)
+        ]
 
     def rows_of(bases, lanes):
         row = lax.broadcasted_iota(jnp.int32, (len(bases), lanes), 0)
         positions = lax.broadcasted_iota(jnp.int32, (len(bases), lanes), 1)
         for i, base in enumerate(bases):
             positions = positions + jnp.where(row == i, base, 0)
-        return ids_of(positions)
-
-    for group in starts:
-        rest.pop(0)[...] = rows_of(group, CHUNK)
-    rest.pop(0)[...] = rows_of([first + i * Q_TILE for i in range(tokens // Q_TILE)], Q_TILE)
+        return positions
+
+    arrays = [rows_of(group, CHUNK) for group in starts]
+    arrays.append(rows_of([first + i * Q_TILE for i in range(tokens // Q_TILE)], Q_TILE))
     strips = tokens // STRIP
     for extra in (0, 1):
         bases = [first + i * STRIP - STRIP // 2 for i in range(-extra, strips + extra)]
-        rest.pop(0)[...] = rows_of(bases, 2 * STRIP)
+        arrays.append(rows_of(bases, 2 * STRIP))
+    for ids in ids_of(arrays):
+        rest.pop(0)[...] = ids
     col_ref = rest.pop(0)
 
     def fill(strip, carry):
-        row = lax.broadcasted_iota(jnp.int32, (STRIP, PAIR), 0)
-        rows = pl.ds(pl.multiple_of(strip * STRIP, STRIP), STRIP)
-        col_ref[rows, :] = ids_of(row + (first + (strip - 2) * STRIP))
+        row = lax.broadcasted_iota(jnp.int32, (2 * STRIP, PAIR), 0)
+        rows = pl.ds(pl.multiple_of(strip * 2 * STRIP, STRIP), 2 * STRIP)
+        col_ref[rows, :] = ids_of([row + (first + (strip - 1) * 2 * STRIP)])[0]
         return carry
 
-    lax.fori_loop(0, strips + 4, fill, 0)
+    lax.fori_loop(0, strips // 2 + 2, fill, 0)
 
 
 def plan(lengths, tokens, groups):
@@ -1272,15 +1281,15 @@
     )
     near_came = swapped(dx_other, "tp")
     occ_local = occupancy(after(key_unit, near_dx), hyperplanes, 2.0**BITS / all_tokens)
-    far_came, near_came, grad_up, down_out = after(
-        (far_came, near_came, grad_up, down_out), occ_local
-    )
+    far_came, near_came = after((far_came, near_came), occ_local)
     count = lax.axis_size("seq")
     low_pair = both_sides(far_dx, far_came, 0, 2)
     high_pair = both_sides(far_dx, far_came, 2, 2)
-    two_low, one_low, one_high, two_high = [
-        both_sides(near_dx, near_came, i, 1) for i in range(len(near))
-    ]
+    near_terms = [both_sides(near_dx, near_came, i, 1) for i in range(len(near))]
+    low_pair, high_pair, near_terms, grad_up, down_out = after(
+        (low_pair, high_pair, near_terms, grad_up, down_out), occ_local
+    )
+    two_low, one_low, one_high, two_high = near_terms
     low_far = shifted(low_pair, "seq", -far_reach)
     high_far = shifted(high_pair, "seq", far_reach)
     last = count - far_reach

time: 702 us -> 694 us (0.989); the launches traced: 705 us -> 681 us
  waiting for transfers between devices: 237 us -> 203 us
  Pallas kernels: 305 us -> 314 us
    psum x1, waiting for transfers between devices: 205 us -> 180 us  [body(): grad_up, down_out = lax.psum((grad_up_low, down_out_low), 'seq')]
    ppermute x14, waiting for transfers between devices: 24.9 us -> 15.2 us  [shifted(): return lax.ppermute(block, axis, route)]
    pallas_call x3, Pallas kernels: 57.2 us -> 64.9 us  [attend(): pl.pallas_call(partial(attend_kernel, head_dim, tiles_k, seed is not None...]
    unnamed x107 -> x117, local copies, waits for them, and re-layouts: 17.9 us -> 19.7 us
  transfers between devices with their start and end apart: 31 -> 31, of which waited for: 10 -> 7; matrix products, arithmetic and copies ran while one was open for 5% -> 6% of each run, Pallas kernels for 38% -> 41%
where the time goes in v2:
time: 694 us; the launch traced here: 681 us
  Pallas kernels  314 us (45%)
  waiting for transfers between devices  203 us (29%)
  starting transfers between devices  50.6 us (7%)
  other arithmetic  43.4 us (6%)
  local copies, waits for them, and re-layouts  36.3 us (5%)
  matrix products  17.9 us (3%)
  between operations  15.6 us (2%)
    psum x1, waiting for transfers between devices, body(): grad_up, down_out = lax.psum((grad_up_low, down_out_low), 'seq')  180 us
    pallas_call x3, Pallas kernels, attend(): pl.pallas_call(partial(attend_kernel, head_dim, tiles_k, seed is not None...  64.9 us
    pallas_call x1, Pallas kernels, sum_over_seq(): pl.pallas_call(partial(sum_kernel, n, streams, split), in_specs=[in_vmem,...  61.2 us
    pallas_call x3, Pallas kernels, back_attend(): pl.pallas_call(partial(back_attend_kernel, head_dim, tiles_k, seed is not...  54.5 us
    ppermute x14, starting transfers between devices, shifted(): return lax.ppermute(block, axis, route)  45.4 us
    pallas_call x3, Pallas kernels, back_project(): pl.pallas_call(partial(back_project_kernel, len(parts), turned, len(value...  43.3 us
    pallas_call x3, Pallas kernels, project(): pl.pallas_call(partial(project_kernel, units, count, head_dim), grid_spec...  24.7 us
    pallas_call x1, Pallas kernels, occupancy(): pl.pallas_call(partial(occupancy_kernel, hashes), grid=(pairs, tokens //...  19.7 us
  transfers between devices with their start and end apart: 31, of which 7 were waited for; matrix products, arithmetic and copies ran while one was open for 6% of the time, Pallas kernels for 41%

profile of v2, /device:TPU:0, one launch (start us, length us, event | category | flops | bytes accessed | tf_op | source)
XLA Modules:
  0.0 681.5 jit_solution(12689744963935670151)
XLA Ops:
  7.3 2.5 constant_dynamic-slice_fusion
  12.4 5.5 collective-permute-start.2
  17.9 4.6 collective-permute-start.1
  22.5 11.2 %plan.1 = (s32[29]{0:T(128)}, s32[33]{0:T(128)}, s32[24]{0:T(128)}, s32[16]{0:T(128)}, s32[8]{0:T(128)}, /*index=5*/s32[29]{0:T(128)}, s32[33]{0:T(128)}, s32[24...) custom-call(s32[32]{0:T(128)} %length_ref.1), custom_call_target="tpu_custom_call" | custom-call | flops 1048576 | bytes 65536 | tf_op jit(solution)/shard_map/plan/pallas_call | solution.py:1102
  36.2 7.4 %project.3 = (bf16[1024,384]{1,0:T(8,128)(2,1)}, f32[1024,384]{1,0:T(8,128)}, bf16[1024,384]{1,0:T(8,128)(2,1)}, f32[1024,384]{1,0:T(8,128)}, bf16[1024,384]{1,0:T(8,128)(2,1)}) custom-call(s32[4]{0:T(128)} %constant.121.clone.table, bf16[1024,768]{1,0:T(8,128)(2,1)} %refs_0_.1, bf16[768,1152]{1,0:T(8,128)(2,1)} %copy-done.11), custom_call_target="tpu_custom_call" | custom-call | flops 3623878656 | bytes 786432 | tf_op jit(solution)/shard_map/project/pallas_call | solution.py:138
  43.6 31.5 %attend.3 = (f32[384,1024]{1,0:T(8,128)}, bf16[6,1024,1024]{2,1,0:T(8,128)(2,1)}) custom-call(s32[11]{0:T(128)} %get-tuple-element.115.table, bf16[1024,384]{1,0:T(8,128)(2,1)} %get-tuple-element.111.q_ref.refs_3_, s32[2,512]{1,0:T(2,128)} %get-tuple-element.112.qrow_ref, s32[2,512]{1,0:T(2,128)} %get-tuple-element.116.krow_ref, ...), custom_call_target="tpu_custom_call" | custom-call | flops 12884901888 | bytes 1572864 | tf_op jit(solution)/shard_map/attend/pallas_call | solution.py:252
  76.3 3.2 collective-permute-start
  82.2 7.6 %collective-permute-start.5 = (bf16[512,768]{1,0:T(8,128)(2,1)S(1)}, bf16[512,768]{1,0:T(8,128)(2,1)}, u32[]{:S(2)}, u32[]{:S(2)}) collective-permute-start(bf16[512,768]{1,0:T(8,128)(2,1)S(1)} %get-tuple-element.120.refs_0_), channel_id=1, source_target_pairs={{0,6},{2,8},{4,10},{6,12},{8,14},{10,16},{12,18},{14,20},{16,22},{... | collective-permute-start | bytes 2359304 | tf_op jit(solution)/shard_map/ppermute | solution.py:1119
  91.6 10.0 %project.4 = (bf16[4608,384]{1,0:T(8,128)(2,1)}, f32[4608,384]{1,0:T(8,128)}, bf16[4608,384]{1,0:T(8,128)(2,1)}) custom-call(s32[16]{0:T(128)} %get-tuple-element.123.table, bf16[512,768]{1,0:T(8,128)(2,1)} %copy-done.35, bf16[512,768]{1,0:T(8,128)(2,1)} %copy-done.34, bf16[512,768]{1,0:T(8,128)(2,1)} %copy-done.33, bf16[512,768]{1,0:T(8,128)(2,1)} %copy-done.32, ...), custom_call_target="tpu_custom_call" | custom-call | flops 9663676416 | bytes 3145728 | tf_op jit(solution)/shard_map/project/pallas_call | solution.py:138
  101.6 23.9 %attend.4 = (f32[384,1024]{1,0:T(8,128)}, bf16[6,4096,1024]{2,1,0:T(8,128)(2,1)}) custom-call(s32[29]{0:T(128)} %get-tuple-element.121.table, bf16[1024,384]{1,0:T(8,128)(2,1)} %get-tuple-element.111.q_ref.refs_3_, s32[2,512]{1,0:T(2,128)} %get-tuple-element.112.qrow_ref, s32[8,512]{1,0:T(8,128)} %get-tuple-element.122.krow_ref, ...), custom_call_target="tpu_custom_call" | custom-call | flops 51539607552 | bytes 1572864 | tf_op jit(solution)/shard_map/attend/pallas_call | solution.py:252
  133.2 7.4 %project.5 = (bf16[4608,384]{1,0:T(8,128)(2,1)}, f32[4608,384]{1,0:T(8,128)}, bf16[4608,384]{1,0:T(8,128)(2,1)}) custom-call(s32[16]{0:T(128)} %get-tuple-element.114.table, bf16[512,768]{1,0:T(8,128)(2,1)} %collective-permute-done.refs_0_, bf16[512,768]{1,0:T(8,128)(2,1)} %collective-permute-done.5.refs_1_, ...), custom_call_target="tpu_custom_call" | custom-call | flops 9663676416 | bytes 3145728 | tf_op jit(solution)/shard_map/project/pallas_call | solution.py:138
  140.6 9.5 %attend.5 = (f32[384,1024]{1,0:T(8,128)}, bf16[6,4096,1024]{2,1,0:T(8,128)(2,1)}) custom-call(s32[29]{0:T(128)} %get-tuple-element.110.table, bf16[1024,384]{1,0:T(8,128)(2,1)} %get-tuple-element.111.q_ref.refs_3_, s32[2,512]{1,0:T(2,128)} %get-tuple-element.112.qrow_ref, s32[8,512]{1,0:T(8,128)} %get-tuple-element.113.krow_ref, ...), custom_call_target="tpu_custom_call" | custom-call | flops 51539607552 | bytes 1572864 | tf_op jit(solution)/shard_map/attend/pallas_call | solution.py:252
  150.1 8.2 %mix.1 = bf16[1024,384]{1,0:T(8,128)(2,1)} custom-call(f32[384,1024]{1,0:T(8,128)} %get-tuple-element.137.g_ref, s32[1536,128]{1,0:T(8,128)} %get-tuple-element.138.col_ref, bf16[1024,384]{1,0:T(8,128)(2,1)} %get-tuple-element.118.v_ref, bf16[32,384]{1,0:T(8,128)(2,1)} %slice_select_fusion.1.rim_ref, s32[8,256]{1,0:T(8,128)} %get-tuple-element.140.row_ref, ...), custom_call_target="tpu_custom_call" | custom-call | flops 1048576 | bytes 65536 | tf_op jit(solution)/shard_map/mix/pallas_call | solution.py:537
  158.3 2.1 convolution_convert_fusion.2
  160.6 3.3 collective-permute-done.16
  167.0 12.8 %feed.1 = (bf16[1024,768]{1,0:T(8,128)(2,1)}, bf16[1024,1536]{1,0:T(8,128)(2,1)}, bf16[1024,1536]{1,0:T(8,128)(2,1)}) custom-call(bf16[1024,768]{1,0:T(8,128)(2,1)} %fusion.4.x_ref, bf16[768,1536]{1,0:T(8,128)(2,1)} %up_ref.1, bf16[1536,768]{1,0:T(8,128)(2,1)} %down_ref.1), custom_call_target="tpu_custom_call" | custom-call | flops 1048576 | bytes 65536 | tf_op jit(solution)/shard_map/feed/pallas_call | solution.py:778
  180.0 3.5 collective-permute-done.17
  183.4 2.6 fusion.18
  188.8 2.6 fusion.17
  191.9 3.0 multiply_convert_fusion
  194.9 2.6 convolution_convert_fusion.3
  197.8 4.2 convolution_convert_fusion.1
  202.0 3.3 convolution_convert_fusion
  205.3 2.1 multiply_reduce_fusion
  211.6 1.9 convolution_convert_fusion.4.m_ref
  217.3 3.6 back_norm.1.g_ref
  220.8 10.6 %back_attend.3 = (bf16[4096,384]{1,0:T(8,128)(2,1)}, bf16[4096,384]{1,0:T(8,128)(2,1)}, f32[384,1024]{1,0:T(8,128)}) custom-call(s32[33]{0:T(128)} %get-tuple-element.150.table, bf16[1024,384]{1,0:T(8,128)(2,1)} %get-tuple-element.111.q_ref.refs_3_, bf16[1024,384]{1,0:T(8,128)(2,1)} %back_norm.1.g_ref, bf16[4608,384]{1,0:T(8,128)(2,1)} %get-tuple-element.135.k_ref.refs_6_, ...), custom_call_target="tpu_custom_call" | custom-call | flops 1048576 | bytes 65536 | tf_op jit(solution)/shard_map/back_attend/pallas_call | solution.py:349
  231.5 11.0 %back_project.3 = (bf16[2048,768]{1,0:T(8,128)(2,1)}, bf16[2048,768]{1,0:T(8,128)(2,1)}, f32[768,768]{1,0:T(8,128)}) custom-call(s32[24]{0:T(128)} %get-tuple-element.148.table, bf16[512,768]{1,0:T(8,128)(2,1)} %collective-permute-done.refs_0_, bf16[512,768]{1,0:T(8,128)(2,1)} %collective-permute-done.5.refs_1_, ...), custom_call_target="tpu_custom_call" | custom-call | flops 1048576 | bytes 65536 | tf_op jit(solution)/shard_map/back_project/pallas_call | solution.py:455
  242.5 10.2 %back_conv.1 = (f32[1280,384]{1,0:T(8,128)}, f32[8,256]{1,0:T(8,128)}) custom-call(s32[1536,128]{1,0:T(8,128)} %get-tuple-element.138.col_ref, bf16[1024,384]{1,0:T(8,128)(2,1)} %get-tuple-element.118.v_ref, bf16[32,384]{1,0:T(8,128)(2,1)} %slice_select_fusion.1.rim_ref, bf16[1024,384]{1,0:T(8,128)(2,1)} %convolution_convert_fusion.4.m_ref, ...), custom_call_target="tpu_custom_call" | custom-call | flops 1048576 | bytes 65536 | tf_op jit(solution)/shard_map/back_conv/pallas_call | solution.py:632
  252.6 17.7 %back_attend.4 = (bf16[4096,384]{1,0:T(8,128)(2,1)}, bf16[4096,384]{1,0:T(8,128)(2,1)}, f32[384,1024]{1,0:T(8,128)}) custom-call(s32[33]{0:T(128)} %get-tuple-element.158.table, bf16[1024,384]{1,0:T(8,128)(2,1)} %get-tuple-element.111.q_ref.refs_3_, bf16[1024,384]{1,0:T(8,128)(2,1)} %back_norm.1.g_ref, bf16[4608,384]{1,0:T(8,128)(2,1)} %get-tuple-element.128.k_ref.refs_6_, ...), custom_call_target="tpu_custom_call" | custom-call | flops 1048576 | bytes 65536 | tf_op jit(solution)/shard_map/back_attend/pallas_call | solution.py:349
  271.1 16.8 %back_project.4 = (bf16[2048,768]{1,0:T(8,128)(2,1)}, bf16[2048,768]{1,0:T(8,128)(2,1)}, f32[768,768]{1,0:T(8,128)}) custom-call(s32[24]{0:T(128)} %get-tuple-element.156.table, bf16[512,768]{1,0:T(8,128)(2,1)} %copy-done.35, bf16[512,768]{1,0:T(8,128)(2,1)} %copy-done.34, bf16[512,768]{1,0:T(8,128)(2,1)} %copy-done.33, bf16[512,768]{1,0:T(8,128)(2,1)} %copy-done.32, ...), custom_call_target="tpu_custom_call" | custom-call | flops 1048576 | bytes 65536 | tf_op jit(solution)/shard_map/back_project/pallas_call | solution.py:455
  290.7 19.7 %occupancy.1 = f32[6,32,256]{2,1,0:T(8,128)} custom-call(bf16[1024,384]{1,0:T(8,128)(2,1)} %get-tuple-element.169.k_ref.refs_6_, bf16[2,128,1024]{2,1,0:T(8,128)(2,1)} %pad_maximum_fusion.3.w_ref), custom_call_target="tpu_custom_call" | custom-call | flops 12582912000 | bytes 1572864 | tf_op jit(solution)/shard_map/occupancy/pallas_call | solution.py:733
  313.1 4.1 add_convert_fusion.7
  317.2 3.9 add_convert_fusion
  321.1 180.3 %all-reduce.8.cloned.1.call-done = (bf16[768,1536]{1,0:T(8,128)(2,1)}, bf16[1920,768]{1,0:T(8,128)(2,1)}) async-done(((bf16[768,1536]{1,0:T(8,128)(2,1)}, bf16[1920,768]{1,0:T(8,128)(2,1)}), (bf16[768,1536]{1,0:T(8,128)(2,1)}, bf16[1920,768]{1,0:T(8,128)(2,1)})) %all-reduce.8.cloned.1.call-update) | async-done | bytes 5308432 | tf_op jit(solution)/shard_map/psum | solution.py:1242
  502.6 5.4 collective-permute-start.25
  509.4 4.6 collective-permute-start.22
  514.0 2.1 slice_select_fusion
  517.5 26.1 %back_attend.5 = (bf16[1024,384]{1,0:T(8,128)(2,1)}, bf16[1024,384]{1,0:T(8,128)(2,1)}, f32[384,1024]{1,0:T(8,128)}) custom-call(s32[15]{0:T(128)} %get-tuple-element.145.table, bf16[1024,384]{1,0:T(8,128)(2,1)} %get-tuple-element.111.q_ref.refs_3_, bf16[1024,384]{1,0:T(8,128)(2,1)} %back_norm.1.g_ref, bf16[1024,384]{1,0:T(8,128)(2,1)} %get-tuple-element.169.k_ref.refs_6_, ...), custom_call_target="tpu_custom_call" | custom-call | flops 34359738368 | bytes 1048576 | tf_op jit(solution)/shard_map/back_attend/pallas_call | solution.py:349
  543.6 13.6 %collective-permute-done.21 = bf16[1024,768]{1,0:T(8,128)(2,1)S(1)} collective-permute-done((bf16[1024,768]{1,0:T(8,128)(2,1)}, bf16[1024,768]{1,0:T(8,128)(2,1)S(1)}, u32[]{:S(2)}, u32[]{:S(2)}) %collective-permute-start.21) | collective-permute-done | bytes 1572896 | tf_op jit(solution)/shard_map/ppermute | solution.py:1119
  560.9 5.5 collective-permute-start.28
  566.3 15.5 %back_project.5 = (bf16[512,768]{1,0:T(8,128)(2,1)}, bf16[512,768]{1,0:T(8,128)(2,1)}, f32[768,1152]{1,0:T(8,128)}) custom-call(s32[6]{0:T(128)} %get-tuple-element.143.table, bf16[512,768]{1,0:T(8,128)(2,1)} %copy-done.12, bf16[512,768]{1,0:T(8,128)(2,1)} %get-tuple-element.234.refs_1_, bf16[768,1152]{1,0:T(8,128)(2,1)} %copy-done.11, ...), custom_call_target="tpu_custom_call" | custom-call | flops 1048576 | bytes 65536 | tf_op jit(solution)/shard_map/back_project/pallas_call | solution.py:455
  582.9 2.3 concatenate.49
  587.0 2.5 slice.193
  589.6 3.0 convert_element_type.266
  598.8 3.1 convert_add_fusion
  602.4 61.2 %sum_over_seq.1 = (f32[768,384]{1,0:T(8,128)}, f32[768,384]{1,0:T(8,128)}, f32[768,384]{1,0:T(8,128)}, f32[128,512]{1,0:T(8,128)}) custom-call(bf16[768,1152]{1,0:T(8,128)(2,1)} %pad_maximum_fusion.2.refs_0_, f32[128,512]{1,0:T(8,128)} %reshape.195.refs_1_), custom_call_target="tpu_custom_call" | custom-call | flops 68719476736 | bytes 16777216 | tf_op jit(solution)/shard_map/sum_over_seq/pallas_call | solution.py:950
  669.3 1.9 pad_maximum_fusion
  (249 shorter events, 65.0 us)
Async XLA Ops:
  7.2 151.1 %copy-start = (bf16[384,768]{1,0:T(8,128)(2,1)S(1)}, bf16[384,768]{1,0:T(8,128)(2,1)}, u32[]{:S(2)}) copy-start(bf16[384,768]{1,0:T(8,128)(2,1)} %param.21) | copy-start | bytes 1769476
  7.2 26.5 %copy-start.39 = (bf16[768,384]{1,0:T(8,128)(2,1)S(1)}, bf16[768,384]{1,0:T(8,128)(2,1)}, u32[]{:S(2)}) copy-start(bf16[768,384]{1,0:T(8,128)(2,1)} %param.19) | copy-start | bytes 1769476
  7.2 494.2 %all-reduce.8.cloned.1.call-start = ((), (), s32[]{:S(2)}) async-start(), calls=%async_computation | async-start | bytes 10616832 | tf_op jit(solution)/shard_map/psum | solution.py:1242
  7.3 26.4 %copy-start.41 = (bf16[768,384]{1,0:T(8,128)(2,1)S(1)}, bf16[768,384]{1,0:T(8,128)(2,1)}, u32[]{:S(2)}) copy-start(bf16[768,384]{1,0:T(8,128)(2,1)} %param.18) | copy-start | bytes 1769476
  9.8 72.4 %copy-start.12 = (bf16[512,768]{1,0:T(8,128)(2,1)}, bf16[512,768]{1,0:T(8,128)(2,1)S(1)}, u32[]{:S(2)}) copy-start(bf16[512,768]{1,0:T(8,128)(2,1)S(1)} %get-tuple-element.120.refs_0_) | copy-start | bytes 2359300
  9.8 65.4 %collective-permute-start.4 = (bf16[512,768]{1,0:T(8,128)(2,1)S(1)}, bf16[512,768]{1,0:T(8,128)(2,1)S(1)}, u32[]{:S(2)}, u32[]{:S(2)}) collective-permute-start(bf16[512,768]{1,0:T(8,128)(2,1)S(1)} %get-tuple-element.120.refs_0_), channel_id=1, source_target_pairs={{4,0},{6,2},{8,4},{10,6},{12,8},{14,10},{16,12},{18,14},{20,16},{2... | collective-permute-start | bytes 2359304 | tf_op jit(solution)/shard_map/ppermute | solution.py:1119
  11.1 64.1 %collective-permute-start.3 = (bf16[512,768]{1,0:T(8,128)(2,1)S(1)}, bf16[512,768]{1,0:T(8,128)(2,1)S(1)}, u32[]{:S(2)}, u32[]{:S(2)}) collective-permute-start(bf16[512,768]{1,0:T(8,128)(2,1)S(1)} %get-tuple-element.120.refs_0_), channel_id=1, source_target_pairs={{2,0},{4,2},{6,4},{8,6},{10,8},{12,10},{14,12},{16,14},{18,16},{20... | collective-permute-start | bytes 2359304 | tf_op jit(solution)/shard_map/ppermute | solution.py:1119
  12.4 62.8 %collective-permute-start.2 = (bf16[512,768]{1,0:T(8,128)(2,1)S(1)}, bf16[512,768]{1,0:T(8,128)(2,1)S(1)}, u32[]{:S(2)}, u32[]{:S(2)}) collective-permute-start(bf16[512,768]{1,0:T(8,128)(2,1)S(1)} %get-tuple-element.120.refs_0_), channel_id=1, source_target_pairs={{0,2},{2,4},{4,6},{6,8},{8,10},{10,12},{12,14},{14,16},{16,18},{18... | collective-permute-start | bytes 2359304 | tf_op jit(solution)/shard_map/ppermute | solution.py:1119
  17.9 57.3 %collective-permute-start.1 = (bf16[512,768]{1,0:T(8,128)(2,1)S(1)}, bf16[512,768]{1,0:T(8,128)(2,1)S(1)}, u32[]{:S(2)}, u32[]{:S(2)}) collective-permute-start(bf16[512,768]{1,0:T(8,128)(2,1)S(1)} %get-tuple-element.120.refs_0_), channel_id=1, source_target_pairs={{0,4},{2,6},{4,8},{6,10},{8,12},{10,14},{12,16},{14,18},{16,20},{1... | collective-permute-start | bytes 2359304 | tf_op jit(solution)/shard_map/ppermute | solution.py:1119
  75.1 14.8 %copy-start.32 = (bf16[512,768]{1,0:T(8,128)(2,1)}, bf16[512,768]{1,0:T(8,128)(2,1)S(1)}, u32[]{:S(2)}) copy-start(bf16[512,768]{1,0:T(8,128)(2,1)S(1)} %collective-permute-done.4.refs_3_) | copy-start | bytes 2359300
  75.1 14.8 %copy-start.33 = (bf16[512,768]{1,0:T(8,128)(2,1)}, bf16[512,768]{1,0:T(8,128)(2,1)S(1)}, u32[]{:S(2)}) copy-start(bf16[512,768]{1,0:T(8,128)(2,1)S(1)} %collective-permute-done.3.refs_2_) | copy-start | bytes 2359300
  75.2 14.8 %copy-start.34 = (bf16[512,768]{1,0:T(8,128)(2,1)}, bf16[512,768]{1,0:T(8,128)(2,1)S(1)}, u32[]{:S(2)}) copy-start(bf16[512,768]{1,0:T(8,128)(2,1)S(1)} %collective-permute-done.2.refs_1_) | copy-start | bytes 2359300
  75.2 4.3 collective-permute-start.8
  75.3 5.5 collective-permute-start.9
  75.8 6.4 collective-permute-start.10
  75.8 14.0 %collective-permute-start.11 = (bf16[512,768]{1,0:T(8,128)(2,1)S(1)}, bf16[512,768]{1,0:T(8,128)(2,1)S(1)}, u32[]{:S(2)}, u32[]{:S(2)}) collective-permute-start(bf16[512,768]{1,0:T(8,128)(2,1)S(1)} %collective-permute-done.4.refs_3_), channel_id=1, source_target_pairs={{0,1},{1,0},{2,3},{3,2},{4,5},{5,4},{6,7},{7,6},{8,9},{9,8},{10,11... | collective-permute-start | bytes 2359304 | tf_op jit(solution)/shard_map/ppermute | solution.py:1123
  76.3 49.3 %collective-permute-start = (bf16[512,768]{1,0:T(8,128)(2,1)S(1)}, bf16[512,768]{1,0:T(8,128)(2,1)}, u32[]{:S(2)}, u32[]{:S(2)}) collective-permute-start(bf16[512,768]{1,0:T(8,128)(2,1)S(1)} %get-tuple-element.120.refs_0_), channel_id=1, source_target_pairs={{0,8},{2,10},{4,12},{6,14},{8,16},{10,18},{12,20},{14,22},{16,24},... | collective-permute-start | bytes 2359304 | tf_op jit(solution)/shard_map/ppermute | solution.py:1119
  79.5 46.1 %collective-permute-start.7 = (bf16[512,768]{1,0:T(8,128)(2,1)S(1)}, bf16[512,768]{1,0:T(8,128)(2,1)}, u32[]{:S(2)}, u32[]{:S(2)}) collective-permute-start(bf16[512,768]{1,0:T(8,128)(2,1)S(1)} %get-tuple-element.120.refs_0_), channel_id=1, source_target_pairs={{8,0},{10,2},{12,4},{14,6},{16,8},{18,10},{20,12},{22,14},{24,16},... | collective-permute-start | bytes 2359304 | tf_op jit(solution)/shard_map/ppermute | solution.py:1119
  80.8 44.7 %collective-permute-start.6 = (bf16[512,768]{1,0:T(8,128)(2,1)S(1)}, bf16[512,768]{1,0:T(8,128)(2,1)}, u32[]{:S(2)}, u32[]{:S(2)}) collective-permute-start(bf16[512,768]{1,0:T(8,128)(2,1)S(1)} %get-tuple-element.120.refs_0_), channel_id=1, source_target_pairs={{6,0},{8,2},{10,4},{12,6},{14,8},{16,10},{18,12},{20,14},{22,16},{... | collective-permute-start | bytes 2359304 | tf_op jit(solution)/shard_map/ppermute | solution.py:1119
  82.2 43.4 %collective-permute-start.5 = (bf16[512,768]{1,0:T(8,128)(2,1)S(1)}, bf16[512,768]{1,0:T(8,128)(2,1)}, u32[]{:S(2)}, u32[]{:S(2)}) collective-permute-start(bf16[512,768]{1,0:T(8,128)(2,1)S(1)} %get-tuple-element.120.refs_0_), channel_id=1, source_target_pairs={{0,6},{2,8},{4,10},{6,12},{8,14},{10,16},{12,18},{14,20},{16,22},{... | collective-permute-start | bytes 2359304 | tf_op jit(solution)/shard_map/ppermute | solution.py:1119
  101.6 25.1 %copy-start.51 = (s32[8]{0:T(128)S(1)}, s32[8]{0:T(128)}, u32[]{:S(2)}) copy-start(s32[8]{0:T(128)} %get-tuple-element.139) | copy-start | bytes 100
  101.6 25.3 %copy-start.46 = (f32[6,33]{1,0:T(8,128)S(1)}, f32[6,33]{1,0:T(8,128)}, u32[]{:S(2)}) copy-start(f32[6,33]{1,0:T(8,128)} %param.24) | copy-start | bytes 2380
  125.6 3.4 collective-permute-start.12
  125.7 4.5 collective-permute-start.13
  126.2 4.2 collective-permute-start.14
  126.2 5.3 collective-permute-start.15
  160.4 3.5 collective-permute-start.16
  179.8 3.6 collective-permute-start.17
  197.6 7.7 %collective-permute-start.18 = (bf16[1024,768]{1,0:T(8,128)(2,1)S(1)}, bf16[1024,768]{1,0:T(8,128)(2,1)S(1)}, u32[]{:S(2)}, u32[]{:S(2)}) collective-permute-start(bf16[1024,768]{1,0:T(8,128)(2,1)S(1)} %convolution_convert_fusion.3), channel_id=1, source_target_pairs={{0,1},{1,0},{2,3},{3,2},{4,5},{5,4},{6,7},{7,6},{8,9},{9,8},{10,11... | collective-permute-start | bytes 4718600 | tf_op jit(solution)/shard_map/ppermute | solution.py:1123
  252.6 17.7 %copy-start.24 = (f32[1280,384]{1,0:T(8,128)S(1)}, f32[1280,384]{1,0:T(8,128)}, u32[]{:S(2)}) copy-start(f32[1280,384]{1,0:T(8,128)} %get-tuple-element.161) | copy-start | bytes 5898244
  287.9 23.6 %collective-permute-start.20 = (bf16[2048,768]{1,0:T(8,128)(2,1)}, bf16[2048,768]{1,0:T(8,128)(2,1)S(1)}, u32[]{:S(2)}, u32[]{:S(2)}) collective-permute-start(bf16[2048,768]{1,0:T(8,128)(2,1)} %get-tuple-element.167), channel_id=1, source_target_pairs={{0,1},{1,0},{2,3},{3,2},{4,5},{5,4},{6,7},{7,6},{8,9},{9,8},{10,11... | collective-permute-start | bytes 9437192 | tf_op jit(solution)/shard_map/ppermute | solution.py:1123
  288.3 24.8 %collective-permute-start.19 = (bf16[2048,768]{1,0:T(8,128)(2,1)}, bf16[2048,768]{1,0:T(8,128)(2,1)}, u32[]{:S(2)}, u32[]{:S(2)}) collective-permute-start(bf16[2048,768]{1,0:T(8,128)(2,1)} %get-tuple-element.155), channel_id=1, source_target_pairs={{0,1},{1,0},{2,3},{3,2},{4,5},{5,4},{6,7},{7,6},{8,9},{9,8},{10,11... | collective-permute-start | bytes 9437192 | tf_op jit(solution)/shard_map/ppermute | solution.py:1123
  290.7 22.4 %copy-start.15 = (bf16[2048,768]{1,0:T(8,128)(2,1)S(1)}, bf16[2048,768]{1,0:T(8,128)(2,1)}, u32[]{:S(2)}) copy-start(bf16[2048,768]{1,0:T(8,128)(2,1)} %get-tuple-element.168) | copy-start | bytes 9437188
  501.4 42.2 %collective-permute-start.24 = (bf16[512,768]{1,0:T(8,128)(2,1)}, bf16[512,768]{1,0:T(8,128)(2,1)S(1)}, u32[]{:S(2)}, u32[]{:S(2)}) collective-permute-start(bf16[512,768]{1,0:T(8,128)(2,1)} %get-tuple-element.174), channel_id=1, source_target_pairs={{4,0},{6,2},{8,4},{10,6},{12,8},{14,10},{16,12},{18,14},{20,16},{2... | collective-permute-start | bytes 2359304 | tf_op jit(solution)/shard_map/ppermute | solution.py:1119
  502.6 41.0 %collective-permute-start.25 = (bf16[512,768]{1,0:T(8,128)(2,1)}, bf16[512,768]{1,0:T(8,128)(2,1)}, u32[]{:S(2)}, u32[]{:S(2)}) collective-permute-start(bf16[512,768]{1,0:T(8,128)(2,1)} %get-tuple-element.177), channel_id=1, source_target_pairs={{0,4},{2,6},{4,8},{6,10},{8,12},{10,14},{12,16},{14,18},{16,20},{1... | collective-permute-start | bytes 2359304 | tf_op jit(solution)/shard_map/ppermute | solution.py:1119
  508.1 49.2 %collective-permute-start.21 = (bf16[1024,768]{1,0:T(8,128)(2,1)}, bf16[1024,768]{1,0:T(8,128)(2,1)S(1)}, u32[]{:S(2)}, u32[]{:S(2)}) collective-permute-start(bf16[1024,768]{1,0:T(8,128)(2,1)} %get-tuple-element.172), channel_id=1, source_target_pairs={{8,0},{10,2},{12,4},{14,6},{16,8},{18,10},{20,12},{22,14},{24,16},... | collective-permute-start | bytes 4718600 | tf_op jit(solution)/shard_map/ppermute | solution.py:1119
  509.4 47.9 %collective-permute-start.22 = (bf16[1024,768]{1,0:T(8,128)(2,1)S(1)}, bf16[1024,768]{1,0:T(8,128)(2,1)S(1)}, u32[]{:S(2)}, u32[]{:S(2)}) collective-permute-start(bf16[1024,768]{1,0:T(8,128)(2,1)S(1)} %get-tuple-element.173), channel_id=1, source_target_pairs={{0,8},{2,10},{4,12},{6,14},{8,16},{10,18},{12,20},{14,22},{16,24},... | collective-permute-start | bytes 4718600 | tf_op jit(solution)/shard_map/ppermute | solution.py:1119
  516.2 27.4 %collective-permute-start.23 = (bf16[512,768]{1,0:T(8,128)(2,1)}, bf16[512,768]{1,0:T(8,128)(2,1)}, u32[]{:S(2)}, u32[]{:S(2)}) collective-permute-start(bf16[512,768]{1,0:T(8,128)(2,1)} %slice_select_fusion), channel_id=1, source_target_pairs={{6,0},{24,30},{7,1},{25,31}} | collective-permute-start | bytes 2359304 | tf_op jit(solution)/shard_map/ppermute | solution.py:1296
  517.4 39.8 %copy-start.13 = (bf16[512,768]{1,0:T(8,128)(2,1)S(1)}, bf16[512,768]{1,0:T(8,128)(2,1)}, u32[]{:S(2)}) copy-start(bf16[512,768]{1,0:T(8,128)(2,1)} %get-tuple-element.176) | copy-start | bytes 2359300
  543.6 38.2 %copy-start.36 = (bf16[512,768]{1,0:T(8,128)(2,1)}, bf16[512,768]{1,0:T(8,128)(2,1)S(1)}, u32[]{:S(2)}) copy-start(bf16[512,768]{1,0:T(8,128)(2,1)S(1)} %collective-permute-done.24) | copy-start | bytes 2359300
  557.3 24.6 %copy-start.25 = (bf16[1024,768]{1,0:T(8,128)(2,1)}, bf16[1024,768]{1,0:T(8,128)(2,1)S(1)}, u32[]{:S(2)}) copy-start(bf16[1024,768]{1,0:T(8,128)(2,1)S(1)} %collective-permute-done.21) | copy-start | bytes 4718596
  557.3 24.6 %copy-start.27 = (bf16[1024,768]{1,0:T(8,128)(2,1)}, bf16[1024,768]{1,0:T(8,128)(2,1)S(1)}, u32[]{:S(2)}) copy-start(bf16[1024,768]{1,0:T(8,128)(2,1)S(1)} %collective-permute-done.22) | copy-start | bytes 4718596
  559.6 36.9 %collective-permute-start.27 = (bf16[512,768]{1,0:T(8,128)(2,1)}, bf16[512,768]{1,0:T(8,128)(2,1)}, u32[]{:S(2)}, u32[]{:S(2)}) collective-permute-start(bf16[512,768]{1,0:T(8,128)(2,1)} %add_convert_fusion.6), channel_id=1, source_target_pairs={{2,0},{4,2},{6,4},{8,6},{10,8},{12,10},{14,12},{16,14},{18,16},{20... | collective-permute-start | bytes 2359304 | tf_op jit(solution)/shard_map/ppermute | solution.py:1119
  560.9 37.2 %collective-permute-start.28 = (bf16[512,768]{1,0:T(8,128)(2,1)}, bf16[512,768]{1,0:T(8,128)(2,1)}, u32[]{:S(2)}, u32[]{:S(2)}) collective-permute-start(bf16[512,768]{1,0:T(8,128)(2,1)} %add_convert_fusion.5), channel_id=1, source_target_pairs={{0,2},{2,4},{4,6},{6,8},{8,10},{10,12},{12,14},{14,16},{16,18},{18... | collective-permute-start | bytes 2359304 | tf_op jit(solution)/shard_map/ppermute | solution.py:1119
  566.3 15.6 %copy-start.48 = (f32[8,256]{1,0:T(8,128)S(1)}, f32[8,256]{1,0:T(8,128)}, u32[]{:S(2)}) copy-start(f32[8,256]{1,0:T(8,128)} %get-tuple-element.199) | copy-start | bytes 24580
  566.3 19.6 %copy-start.4 = (bf16[1920,768]{1,0:T(8,128)(2,1)S(1)}, bf16[1920,768]{1,0:T(8,128)(2,1)}, u32[]{:S(2)}) copy-start(bf16[1920,768]{1,0:T(8,128)(2,1)} %get-tuple-element.203) | copy-start | bytes 8847364
  581.9 16.2 %collective-permute-start.26 = (bf16[512,768]{1,0:T(8,128)(2,1)}, bf16[512,768]{1,0:T(8,128)(2,1)}, u32[]{:S(2)}, u32[]{:S(2)}) collective-permute-start(bf16[512,768]{1,0:T(8,128)(2,1)} %get-tuple-element.190), channel_id=1, source_target_pairs={{0,1},{1,0},{2,3},{3,2},{4,5},{5,4},{6,7},{7,6},{8,9},{9,8},{10,11... | collective-permute-start | bytes 2359304 | tf_op jit(solution)/shard_map/ppermute | solution.py:1123
  601.8 65.8 %collective-permute-start.29 = (f32[512,768]{1,0:T(8,128)S(1)}, f32[512,768]{1,0:T(8,128)}, u32[]{:S(2)}, u32[]{:S(2)}) collective-permute-start(f32[512,768]{1,0:T(8,128)S(1)} %convert_add_fusion), channel_id=1, source_target_pairs={{0,1},{1,0},{2,3},{3,2},{4,5},{5,4},{6,7},{7,6},{8,9},{9,8},{10,11... | collective-permute-start | bytes 4718600 | tf_op jit(solution)/shard_map/ppermute | solution.py:1123
  (35 other events, 118.8 us)
Sparse Core Ops, SparseCore 0:
  215.5 285.8 all-reduce.7
